TPU v7x, 128 devices: a whole 4x4x4 slice. The times are simulated.
128 devices in a mesh: row: 8 (over y_lo, z), col: 16 (over y_hi, x, core).
Axes of the slice: x: 4, y: 4 (y_hi: 2, y_lo: 2; y = y_hi * 2 + y_lo), z: 4, core: 2. Of those that a mesh axis runs over, the one named last changes fastest.
Arguments:
- amplitudes: bfloat16 [16384, 16384], P('row', 'col'), may hold values from -0.046875 to 0.046875
- accumulated: float32 [16384, 16384], P('row', 'col'), may hold values from -6 to 6
- cholesky: bfloat16 [16384, 1536], P(('row', 'col')), may hold values from -1.5 to 1.5
- occ_index: int32 [16384], replicated, may hold values from 0 to 63
- vir_index: int32 [16384], replicated, may hold values from 0 to 255
- occ_energy: float32 [64], replicated, may hold values from -3 to -0.5
- vir_energy: float32 [256], replicated, may hold values from 0.5 to 4
Outputs:
- updated: float32 [16384, 16384], P('row', 'col')
All inputs are finite; a program needn't handle non-finite values.
Results may differ from a plain program's by a relative error of at most 0.0022.
Values may be sent and summed in bfloat16 or wider, within the bound.
No kernel may reach another device: no remote copies, remote signals or barrier semaphores. Data moves between devices by JAX's collectives and lax.ppermute only.
A program may use at most 128 MiB of HBM per device.

v0:
```python
import jax
import jax.numpy as jnp
from jax import lax
from jax.sharding import PartitionSpec as P


def spread(value, axis, source):
    kept = jnp.where(lax.axis_index(axis) == source, value, 0).astype(value.dtype)
    return lax.psum(kept, axis)


def lookup(index, table):
    hits = index[:, None] == jnp.arange(table.shape[0], dtype=jnp.int32)[None, :]
    return jnp.sum(jnp.where(hits, table[None, :], jnp.zeros((), table.dtype)), axis=1)


def on_device(amplitudes, accumulated, cholesky, occ_index, vir_index, occ_energy, vir_energy):
    row_count = lax.axis_size("row")
    col_count = lax.axis_size("col")
    ratio = col_count // row_count
    row_rank = lax.axis_index("row")
    col_rank = lax.axis_index("col")
    row_block = amplitudes.shape[0]
    col_block = amplitudes.shape[1]
    owner = col_rank // ratio
    offset = col_rank % ratio * col_block
    b_rows = lax.all_gather(cholesky, "col", axis=0, tiled=True)
    b_half = lax.dynamic_slice_in_dim(b_rows, offset, col_block, 0)
    b_cols = spread(b_half, "row", owner)
    partial_value = jnp.dot(amplitudes, b_cols, preferred_element_type=jnp.float32)
    summed = lax.psum(partial_value, "col")
    x_rows = (b_rows.astype(jnp.float32) + summed).astype(jnp.bfloat16)
    x_half = lax.dynamic_slice_in_dim(x_rows, offset, col_block, 0)
    x_cols = spread(x_half, "row", owner)
    product = lax.dot_general(
        x_rows, x_cols, (((1,), (1,)), ((), ())), preferred_element_type=jnp.float32
    )
    occ_rows = lax.dynamic_slice_in_dim(occ_index, row_rank * row_block, row_block, 0)
    vir_rows = lax.dynamic_slice_in_dim(vir_index, row_rank * row_block, row_block, 0)
    occ_cols = lax.dynamic_slice_in_dim(occ_index, col_rank * col_block, col_block, 0)
    vir_cols = lax.dynamic_slice_in_dim(vir_index, col_rank * col_block, col_block, 0)
    gap_rows = lookup(occ_rows, occ_energy) - lookup(vir_rows, vir_energy)
    gap_cols = lookup(occ_cols, occ_energy) - lookup(vir_cols, vir_energy)
    return accumulated + product / (gap_rows[:, None] + gap_cols[None, :])


def solution(mesh):
    in_specs = (P("row", "col"), P("row", "col"), P(("row", "col"), None), P(), P(), P(), P())
    out_specs = P("row", "col")
    return jax.shard_map(
        on_device, mesh=mesh, in_specs=in_specs, out_specs=out_specs, check_vma=False
    )
```

profile of v0, /device:TPU:0, one launch (start us, length us, event | category | flops | bytes accessed | tf_op | source)
XLA Modules:
  0.0 490.9 jit_solution(18163376625999686682)
XLA Ops:
  6.5 0.0 all-gather.2.cloned.1.call-start
  6.5 1.9 copy.9
  8.5 0.0 all-gather.2.cloned.1.call-update
  8.5 0.0 all-reduce.4.cloned.1.call-start
  8.6 72.2 %all-gather.2.cloned.1.call-done = bf16[2048,1536]{0,1:T(8,128)(2,1)} async-done(((bf16[128,1536]{0,1:T(8,128)(2,1)}), bf16[2048,1536]{0,1:T(8,128)(2,1)}) %all-gather.2.cloned.1.call-update) | async-done | bytes 6291472 | tf_op jit(solution)/shard_map/all_gather | solution.py:27
  80.7 4.4 dynamic-slice_select_fusion.1
  85.2 0.0 all-reduce.4.cloned.1.call-update
  85.2 0.0 all-reduce.6.cloned.1.call-start
  85.2 89.5 %all-reduce.4.cloned.1.call-done = bf16[1024,1536]{0,1:T(8,128)(2,1)} async-done(((bf16[1024,1536]{0,1:T(8,128)(2,1)}), bf16[1024,1536]{0,1:T(8,128)(2,1)}) %all-reduce.4.cloned.1.call-update) | async-done | bytes 3145744 | tf_op jit(solution)/shard_map/psum | solution.py:9
  174.7 12.2 %convolution_bitcast_fusion = f32[2048,1536]{0,1:T(8,128)} fusion(bf16[1024,1536]{0,1:T(8,128)(2,1)} %all-reduce.4.cloned.1.call-done, bf16[2048,1024]{1,0:T(8,128)(2,1)} %param.7), kind=kOutput, calls=%fused_computation.1 | convolution fusion | flops 6442450944 | bytes 19922944 | tf_op jit(solution)/shard_map/dot_general | solution.py:30
  186.9 0.0 all-reduce.6.cloned.1.call-update
  186.9 0.0 all-reduce.8.cloned.1.call-start
  187.0 177.1 %all-reduce.6.cloned.1.call-done = f32[2048,1536]{0,1:T(8,128)} async-done(((f32[2048,1536]{0,1:T(8,128)}), f32[2048,1536]{0,1:T(8,128)}) %all-reduce.6.cloned.1.call-update) | async-done | bytes 12582928 | tf_op jit(solution)/shard_map/psum | solution.py:31
  364.0 11.6 %add_convert_fusion = bf16[2048,1536]{0,1:T(8,128)(2,1)} fusion(f32[2048,1536]{0,1:T(8,128)} %all-reduce.6.cloned.1.call-done, bf16[2048,1536]{0,1:T(8,128)(2,1)} %all-gather.2.cloned.1.call-done), kind=kLoop, calls=%fused_computation | loop fusion | flops 9437184 | bytes 25165824 | tf_op jit(solution)/shard_map/convert_element_type | solution.py:32
  375.7 0.0 copy-start.1
  375.7 0.0 copy-start
  375.7 4.5 dynamic-slice_select_fusion
  380.1 0.0 all-reduce.8.cloned.1.call-update
  380.2 0.7 dynamic_slice.23
  380.9 0.7 dynamic_slice.22
  381.6 0.7 dynamic_slice.21
  382.3 0.7 dynamic_slice.20
  383.0 0.0 copy-done.1
  383.0 0.1 select_reduce_fusion.3
  383.1 0.0 copy-done
  383.1 0.4 select_reduce_fusion.1
  383.5 0.2 select_reduce_fusion.2
  383.6 0.7 select_reduce_fusion
  384.4 86.5 %all-reduce.8.cloned.1.call-done = bf16[1024,1536]{0,1:T(8,128)(2,1)} async-done(((bf16[1024,1536]{0,1:T(8,128)(2,1)}), bf16[1024,1536]{0,1:T(8,128)(2,1)}) %all-reduce.8.cloned.1.call-update) | async-done | bytes 3145744 | tf_op jit(solution)/shard_map/psum | solution.py:9
  470.9 13.5 %divide_add_fusion = f32[2048,1024]{1,0:T(8,128)} fusion(f32[2048,1024]{1,0:T(8,128)} %param.8, f32[1024]{0:T(1024)S(1)} %sub.20, f32[2048]{0:T(1024)S(1)} %sub.19, bf16[2048,1536]{0,1:T(8,128)(2,1)} %add_convert_fusion, bf16[1024,1536]{0,1:T(8,128)(2,1)} %all-reduce.8.cloned.1.call-done), kind=kOutput, calls=%fused_computation.2 | convolution fusion | flops 6448742400 | bytes 26226688 | tf_op jit(solution)/shard_map/dot_general | solution.py:35
  (2 shorter events, 0.0 us)
Async XLA Ops:
  6.5 74.2 %all-gather.2.cloned.1.call-start = ((), (), s32[]{:S(2)}) async-start(), calls=%async_computation | async-start | bytes 6684672 | tf_op jit(solution)/shard_map/all_gather | solution.py:27
  8.5 166.3 %all-reduce.4.cloned.1.call-start = ((), (), s32[]{:S(2)}) async-start(), calls=%async_computation.1 | async-start | bytes 6291456 | tf_op jit(solution)/shard_map/psum | solution.py:9
  85.2 278.9 %all-reduce.6.cloned.1.call-start = ((), (), s32[]{:S(2)}) async-start(), calls=%async_computation.2 | async-start | bytes 25165824 | tf_op jit(solution)/shard_map/psum | solution.py:31
  186.9 283.9 %all-reduce.8.cloned.1.call-start = ((), (), s32[]{:S(2)}) async-start(), calls=%async_computation.3 | async-start | bytes 6291456 | tf_op jit(solution)/shard_map/psum | solution.py:9
  375.7 7.3 %copy-start.1 = (f32[64]{0:T(128)S(1)}, f32[64]{0:T(128)}, u32[]{:S(2)}) copy-start(f32[64]{0:T(128)} %param.12) | copy-start | bytes 772
  375.7 7.4 %copy-start = (f32[256]{0:T(256)S(1)}, f32[256]{0:T(256)}, u32[]{:S(2)}) copy-start(f32[256]{0:T(256)} %param.13) | copy-start | bytes 3076
Sparse Core Ops, SparseCore 0:
  9.6 71.0 all-gather.1
  85.3 89.3 all-reduce.3
  187.1 176.9 all-reduce.5
  380.3 90.5 all-reduce.7
where the time goes:
time: 491 us
  waiting for transfers between devices  425 us (87%)
  matrix products  25.6 us (5%)
  other arithmetic  21.9 us (4%)
  between operations  13.2 us (3%)
    psum x1, waiting for transfers between devices, on_device(): summed = lax.psum(partial_value, 'col')  177 us
    psum x2, waiting for transfers between devices, spread(): return lax.psum(kept, axis)  176 us
    all_gather x1, waiting for transfers between devices, on_device(): b_rows = lax.all_gather(cholesky, 'col', axis=0, tiled=True)  72.2 us
    dot_general x1, matrix products, on_device(): lax.dot_general(x_rows, x_cols, (((1,), (1,)), ((), ())), preferred_eleme...  13.5 us
    dot_general x1, matrix products, on_device(): jnp.dot(amplitudes, b_cols, preferred_element_type=jnp.float32)  12.2 us
    convert_element_type x1, other arithmetic, on_device(): x_rows = (b_rows.astype(jnp.float32) + summed).astype(jnp.bfloat16)  11.6 us
  transfers between devices with their start and end apart: 4, of which 4 were waited for; matrix products, arithmetic and copies ran while one was open for 1% of the time, Pallas kernels for 0%

commit v1 on v0

v1 whole, which is shorter than its diff:
```python
import functools

import jax
import jax.numpy as jnp
from jax import lax
from jax.experimental import pallas as pl
from jax.experimental.pallas import tpu as pltpu
from jax.sharding import PartitionSpec as P


WIDTHS = (256, 512)
ORDER = "SsRrYyQq*FfPpXUxONuZWnowzGVvgEe"
SCALE = 64.0

PLACES = [(x, h, l, z, c) for x in range(4) for h in range(2) for l in range(2) for z in range(4) for c in range(2)]


def index_of(x, h, l, z, c):
    return (l * 4 + z % 4) * 16 + (h * 4 + x % 4) * 2 + c


def send(value, to):
    pairs = [(index_of(*p), index_of(*to(*p))) for p in PLACES if to(*p) is not None]
    return lax.ppermute(value, ("row", "col"), pairs)


def other_core(x, h, l, z, c):
    return x, h, l, z, 1 - c


def other_h(x, h, l, z, c):
    return x, 1 - h, l, z, c


def other_l(x, h, l, z, c):
    return x, h, 1 - l, z, c


def along_x(step):
    return lambda x, h, l, z, c: (x + step, h, l, z, c)


def along_z(step):
    return lambda x, h, l, z, c: (x, h, l, z + step, c)


def along_col(swap, step):
    return lambda x, h, l, z, c: (x + step, h ^ swap, l, z, c)


def skew(x, h, l, z, c):
    return x, h, l, z + x, c


def reflect(x, h, l, z, c):
    return z - x, l, h, z, c


def pass_core(x, h, l, z, c):
    return (x, h, l, z, 1 - c) if l != c else (x, h, 1 - l, z, c)


def cross_core(x, h, l, z, c):
    return (x, h, 1 - l, z, 1 - c) if l != c else None


RING = (0, 1, -1, 2)
SWAP_RING = [(s, r) for s in (0, 1) for r in RING]
TARGETS = [(1, 2), (1, 1), (1, -1), (1, 0), (0, 2), (0, 1), (0, -1), (0, 0)]


def near_sends(base, along):
    return [send(base, along(-1)), send(base, along(1))]


def first_kernel(meta, *refs):
    lefts, pieces, out, held = refs[:4], refs[4:12], refs[12], refs[13]
    rows = pieces[0].shape[0]

    @pl.when(pl.program_id(0) == 0)
    def _():
        for i in range(8):
            held[pl.ds(pl.multiple_of(meta[8 + i] * rows, rows), rows), :] = pieces[i][...]

    own = jnp.concatenate([lefts[0][...], lefts[1][...]], axis=0)
    other = jnp.concatenate([lefts[2][...], lefts[3][...]], axis=0)
    left = jnp.concatenate([own, other], axis=1)
    value = jnp.dot(left, held[...], preferred_element_type=jnp.float32)
    out[0] = value[:rows]
    out[1] = value[rows:]


def first_product(meta, own, other, pieces):
    rows, width = pieces[0].shape
    depth = own.shape[1]
    even = pl.BlockSpec((rows, depth), lambda j, m: (m[2 * j], 0))
    odd = pl.BlockSpec((rows, depth), lambda j, m: (m[2 * j + 1], 0))
    return pl.pallas_call(
        first_kernel,
        out_shape=jax.ShapeDtypeStruct((8, rows, width), jnp.float32),
        grid_spec=pltpu.PrefetchScalarGridSpec(
            num_scalar_prefetch=1,
            grid=(4,),
            in_specs=[even, odd, even, odd] + [pl.BlockSpec((rows, width), lambda j, m: (0, 0))] * 8,
            out_specs=pl.BlockSpec((2, rows, width), lambda j, m: (j, 0, 0)),
            scratch_shapes=[pltpu.VMEM((8 * rows, width), jnp.bfloat16)],
        ),
        cost_estimate=pl.CostEstimate(
            flops=2 * 8 * rows * 2 * depth * width,
            bytes_accessed=8 * rows * (4 * depth + 6 * width),
            transcendentals=0,
        ),
        name="first",
    )(meta, own, own, other, other, *pieces)


def order_rows_kernel(meta, *refs):
    pieces, out = refs[:8], refs[8]
    rows = pieces[0].shape[0]
    for i in range(8):
        out[pl.ds(pl.multiple_of(meta[16 + i] * rows, rows), rows), :] = pieces[i][...]


def order_rows(meta, pieces):
    rows, width = pieces[0].shape
    spec = pl.BlockSpec(memory_space=pltpu.VMEM)
    return pl.pallas_call(
        order_rows_kernel,
        out_shape=jax.ShapeDtypeStruct((8 * rows, width), jnp.bfloat16),
        grid_spec=pltpu.PrefetchScalarGridSpec(
            num_scalar_prefetch=1, grid=(), in_specs=[spec] * 8, out_specs=spec
        ),
        cost_estimate=pl.CostEstimate(flops=0, bytes_accessed=32 * rows * width, transcendentals=0),
        name="order_rows",
    )(meta, *pieces)


def second_kernel(widths, meta, acc_ref, gap_rows_ref, gap_cols_ref, *refs):
    count = len(widths)
    row_refs, col_refs, out_ref, held = refs[:count], refs[count : 5 * count], refs[5 * count], refs[5 * count + 1]
    rows = col_refs[0].shape[0]

    @pl.when(pl.program_id(0) == 0)
    def _():
        start = 0
        for i in range(count):
            for r in range(4):
                place = pl.ds(pl.multiple_of(meta[24 + r] * rows, rows), rows)
                held[place, start : start + widths[i]] = col_refs[4 * i + r][...]
            start += widths[i]

    left = jnp.concatenate([r[...] for r in row_refs], axis=1)
    product = lax.dot_general(left, held[...], (((1,), (1,)), ((), ())), preferred_element_type=jnp.float32)
    out_ref[...] = acc_ref[...] + product / (gap_rows_ref[:, :1] + gap_cols_ref[...])


def second_product(meta, accumulated, gap_rows, gap_cols, row_parts, col_parts):
    rows, cols = accumulated.shape
    widths = [part.shape[1] for part in row_parts]
    depth = sum(widths)
    block = 512
    return pl.pallas_call(
        functools.partial(second_kernel, widths),
        out_shape=jax.ShapeDtypeStruct((rows, cols), jnp.float32),
        grid_spec=pltpu.PrefetchScalarGridSpec(
            num_scalar_prefetch=1,
            grid=(rows // block,),
            in_specs=[
                pl.BlockSpec((block, cols), lambda i, m: (i, 0)),
                pl.BlockSpec((block, 128), lambda i, m: (i, 0)),
                pl.BlockSpec((1, cols), lambda i, m: (0, 0)),
            ]
            + [pl.BlockSpec((block, width), lambda i, m: (i, 0)) for width in widths]
            + [pl.BlockSpec((cols // 4, width), lambda i, m: (0, 0)) for width in widths for _ in range(4)],
            out_specs=pl.BlockSpec((block, cols), lambda i, m: (i, 0)),
            scratch_shapes=[pltpu.VMEM((cols, depth), jnp.bfloat16)],
        ),
        cost_estimate=pl.CostEstimate(
            flops=2 * rows * cols * depth,
            bytes_accessed=rows * cols * 8 + 2 * (rows + cols) * depth,
            transcendentals=0,
        ),
        name="second",
    )(meta, accumulated, gap_rows, gap_cols, *row_parts, *col_parts)


def lookup(index, table):
    hits = index[:, None] == jnp.arange(table.shape[0], dtype=jnp.int32)[None, :]
    return jnp.sum(jnp.where(hits, table[None, :], jnp.zeros((), table.dtype)), axis=1)


def narrow(value):
    return (value * SCALE).astype(jnp.float16)


def widen(value):
    return value.astype(jnp.float32) * (1.0 / SCALE)


class Shared:
    pass


class Chunk:
    def __init__(self, env, b_piece):
        self.env, self.b_piece = env, b_piece

    def S(self):
        self.skewed = send(self.b_piece, skew)

    def R(self):
        self.base = send(self.skewed, reflect)

    def Y(self):
        self.swapped = send(self.base, other_l)
        self.near = near_sends(self.base, along_z)

    def Q(self):
        self.near_swapped = near_sends(self.swapped, along_z)

    def F(self):
        across = send(self.near[1], along_z(1))
        across_swapped = send(self.near_swapped[0], along_z(-1))
        self.b_pieces = [self.base, *self.near, across, self.swapped, *self.near_swapped, across_swapped]

    def P(self):
        self.partials = first_product(self.env.meta, self.env.own, self.env.other, self.b_pieces)
        self.arrived = [send(narrow(self.partials[i]), along_col(*TARGETS[i])) for i in range(7)]

    def X(self):
        total = self.partials[7] + sum(widen(a) for a in self.arrived)
        self.x_piece = (self.b_piece.astype(jnp.float32) + total).astype(jnp.bfloat16)
        self.skewed = send(self.x_piece, skew)
        self.swapped = send(self.x_piece, other_h)

    def O(self):
        self.near = near_sends(self.x_piece, along_x)

    def U(self):
        self.base = send(self.skewed, reflect)

    def W(self):
        self.near_swapped = near_sends(self.swapped, along_x)

    def V(self):
        across = send(self.near[1], along_x(1))
        across_swapped = send(self.near_swapped[0], along_x(-1))
        self.row_pieces = [self.x_piece, *self.near, across, self.swapped, *self.near_swapped, across_swapped]

    def N(self):
        near = send(self.base, pass_core)
        far = send(self.base, cross_core)
        straight = self.env.l == self.env.c
        self.mine = jnp.where(straight, self.base, near)
        self.theirs = jnp.where(straight, near, far)

    def Z(self):
        self.mine_near = near_sends(self.mine, along_z)
        self.theirs_near = near_sends(self.theirs, along_z)

    def G(self):
        mine_across = send(self.mine_near[1], along_z(1))
        theirs_across = send(self.theirs_near[0], along_z(-1))
        self.env.col_mine += [self.mine, *self.mine_near, mine_across]
        self.env.col_theirs += [self.theirs, *self.theirs_near, theirs_across]

    def E(self):
        x_rows = order_rows(self.env.meta, self.row_pieces)
        self.env.row_mine.append(x_rows)
        self.env.row_theirs.append(send(x_rows, other_core))


def on_device(amplitudes, accumulated, cholesky, occ_index, vir_index, occ_energy, vir_energy):
    row_rank = lax.axis_index("row").astype(jnp.int32)
    col_rank = lax.axis_index("col").astype(jnp.int32)
    row_block, col_block = amplitudes.shape
    l, z = row_rank >> 2, row_rank & 3
    h, x, c = col_rank >> 3, (col_rank >> 1) & 3, col_rank & 1
    env = Shared()
    env.l, env.c = l, c

    swap, ring = jnp.array(SWAP_RING, jnp.int32).T
    to_h, to_x = jnp.array(TARGETS, jnp.int32).T
    destinations = (h ^ to_h) * 4 + ((x + to_x) & 3)
    sources = ((l ^ swap) * 4 + ((z + ring - x) & 3) - 4 * c) & 7
    mine = (h ^ swap) * 4 + ((x + ring) & 3)
    env.meta = jnp.concatenate([destinations, sources, mine, (z + ring - x) & 3])

    half = cholesky.shape[1] // 2
    low, high = cholesky[:, :half], cholesky[:, half:]
    keep = jnp.where(c == 0, low, high)
    got = send(jnp.where(c == 0, high, low), other_core)
    b_piece = jnp.concatenate([jnp.where(c == 0, keep, got), jnp.where(c == 0, got, keep)], axis=0)
    env.own = amplitudes

    occ_rows = lax.dynamic_slice_in_dim(occ_index, row_rank * row_block, row_block, 0)
    vir_rows = lax.dynamic_slice_in_dim(vir_index, row_rank * row_block, row_block, 0)
    occ_cols = lax.dynamic_slice_in_dim(occ_index, col_rank * col_block, col_block, 0)
    vir_cols = lax.dynamic_slice_in_dim(vir_index, col_rank * col_block, col_block, 0)
    gap_rows = lookup(occ_rows, occ_energy) - lookup(vir_rows, vir_energy)
    gap_cols = lookup(occ_cols, occ_energy) - lookup(vir_cols, vir_energy)
    env.meta, gap_rows, gap_cols = lax.optimization_barrier(
        (env.meta, jnp.broadcast_to(gap_rows[:, None], (row_block, 128)), gap_cols[None, :])
    )

    env.row_mine, env.row_theirs, env.col_mine, env.col_theirs = [], [], [], []
    starts = [sum(WIDTHS[:j]) for j in range(len(WIDTHS))]
    chunks = [Chunk(env, b_piece[:, start : start + width]) for start, width in zip(starts, WIDTHS)]
    for stage in ORDER:
        if stage == "*":
            env.other = send(amplitudes, other_core)
        else:
            getattr(chunks[int(stage.islower())], stage.upper())()
    return second_product(
        env.meta, accumulated, gap_rows, gap_cols, env.row_mine + env.row_theirs, env.col_mine + env.col_theirs
    )


def solution(mesh):
    in_specs = (P("row", "col"), P("row", "col"), P(("row", "col"), None), P(), P(), P(), P())
    out_specs = P("row", "col")
    return jax.shard_map(on_device, mesh=mesh, in_specs=in_specs, out_specs=out_specs, check_vma=False)
```

time: 491 us -> 257 us (0.52)
  waiting for transfers between devices: 425 us -> 55.3 us
  starting transfers between devices: 0.13 us -> 138 us
  Pallas kernels: 0 us -> 38.4 us
  matrix products: 25.6 us -> 0 us
  between operations: 13.2 us -> 0.87 us
  other arithmetic: 21.9 us -> 13 us
    psum x3 -> x0, waiting for transfers between devices: 353 us -> none  [the longest x1 177 us: on_device(): summed = lax.psum(partial_value, 'col')]
    ppermute x0 -> x70, starting transfers between devices: none -> 138 us  [send(): return lax.ppermute(value, ('row', 'col'), pairs)]
    all_gather x1 -> x0, waiting for transfers between devices: 72.2 us -> none  [on_device(): b_rows = lax.all_gather(cholesky, 'col', axis=0, tiled=True)]
    ppermute x0 -> x70, waiting for transfers between devices: none -> 55.3 us  [send(): return lax.ppermute(value, ('row', 'col'), pairs)]
    pallas_call x0 -> x5, Pallas kernels: none -> 38.4 us  [the longest x2 17.7 us: first_product(): pl.pallas_call(first_kernel, out_shape=jax.ShapeDtypeStruct((8, rows, wid...]
    dot_general x2 -> x0, matrix products: 25.6 us -> none  [the longest x1 13.5 us: on_device(): lax.dot_general(x_rows, x_cols, (((1,), (1,)), ((), ())), preferred_eleme...]
    select_n x2 -> x4, other arithmetic: 8.88 us -> 3.09 us  [the longest x1 1.07 us: on_device(): jnp.where(c == 0, keep, got)]
    convert_element_type x1 -> x4, other arithmetic: 11.6 us -> 7.29 us  [the longest x2 4.83 us: narrow(): return (value * SCALE).astype(jnp.float16)]
  transfers between devices with their start and end apart: 4 -> 70, of which waited for: 4 -> 24; matrix products, arithmetic and copies ran while one was open for 1% -> 7% of each run, Pallas kernels for 0% -> 10%
where the time goes in v1:
time: 257 us; the launch traced here: 255 us
  starting transfers between devices  138 us (54%)
  waiting for transfers between devices  55.3 us (22%)
  Pallas kernels  38.4 us (15%)
  other arithmetic  13 us (5%)
  local copies, waits for them, and re-layouts  9.61 us (4%)
    ppermute x70, starting transfers between devices, send(): return lax.ppermute(value, ('row', 'col'), pairs)  138 us
    ppermute x70, waiting for transfers between devices, send(): return lax.ppermute(value, ('row', 'col'), pairs)  55.3 us
    pallas_call x2, Pallas kernels, first_product(): pl.pallas_call(first_kernel, out_shape=jax.ShapeDtypeStruct((8, rows, wid...  17.7 us
    pallas_call x1, Pallas kernels, second_product(): pl.pallas_call(functools.partial(second_kernel, widths), out_shape=jax.Sh...  14.1 us
    pallas_call x2, Pallas kernels, order_rows(): pl.pallas_call(order_rows_kernel, out_shape=jax.ShapeDtypeStruct((8 * row...  6.61 us
    unnamed x110, local copies, waits for them, and re-layouts  5.51 us
  transfers between devices with their start and end apart: 70, of which 24 were waited for; matrix products, arithmetic and copies ran while one was open for 7% of the time, Pallas kernels for 10%

profile of v1, /device:TPU:0, one launch (start us, length us, event | category | flops | bytes accessed | tf_op | source)
XLA Modules:
  0.0 254.7 jit_solution(517544275962458916)
XLA Ops:
  1.7 6.0 %collective-permute-done = bf16[128,768]{1,0:T(8,128)(2,1)S(1)} collective-permute-done((bf16[128,768]{1,0:T(8,128)(2,1)S(1)}, bf16[128,768]{1,0:T(8,128)(2,1)S(1)}, u32[]{:S(2)}, u32[]{:S(2)}) %collective-permute-start) | collective-permute-done | bytes 196640 | tf_op jit(solution)/shard_map/ppermute | solution.py:24
  12.4 9.1 %collective-permute-start.30 = (bf16[256,512]{1,0:T(8,128)(2,1)S(1)}, bf16[256,512]{1,0:T(8,128)(2,1)S(1)}, u32[]{:S(2)}, u32[]{:S(2)}) collective-permute-start(bf16[256,512]{1,0:T(8,128)(2,1)S(1)} %collective-permute-done.26.refs_4_), channel_id=1, source_target_pairs={{0,64},{1,65},{16,80},{17,81},{32,96},{33,97},{48,112},{49,113},{6... | collective-permute-start | bytes 786440 | tf_op jit(solution)/shard_map/ppermute | solution.py:24
  24.1 11.4 %collective-permute-start.28 = (bf16[256,512]{1,0:T(8,128)(2,1)S(1)}, bf16[256,512]{1,0:T(8,128)(2,1)S(1)}, u32[]{:S(2)}, u32[]{:S(2)}) collective-permute-start(bf16[256,512]{1,0:T(8,128)(2,1)S(1)} %collective-permute-done.26.refs_4_), channel_id=1, source_target_pairs={{0,16},{1,17},{16,32},{17,33},{32,48},{33,49},{48,0},{49,1},{64,80... | collective-permute-start | bytes 786440 | tf_op jit(solution)/shard_map/ppermute | solution.py:24
  35.5 7.1 %collective-permute-start.31 = (bf16[256,512]{1,0:T(8,128)(2,1)S(1)}, bf16[256,512]{1,0:T(8,128)(2,1)S(1)}, u32[]{:S(2)}, u32[]{:S(2)}) collective-permute-start(bf16[256,512]{1,0:T(8,128)(2,1)S(1)} %collective-permute-done.30.refs_8_), channel_id=1, source_target_pairs={{0,48},{1,49},{16,0},{17,1},{32,16},{33,17},{48,32},{49,33},{64,11... | collective-permute-start | bytes 786440 | tf_op jit(solution)/shard_map/ppermute | solution.py:24
  44.1 8.1 %collective-permute-start.27 = (bf16[256,512]{1,0:T(8,128)(2,1)S(1)}, bf16[256,512]{1,0:T(8,128)(2,1)S(1)}, u32[]{:S(2)}, u32[]{:S(2)}) collective-permute-start(bf16[256,512]{1,0:T(8,128)(2,1)S(1)} %collective-permute-done.26.refs_4_), channel_id=1, source_target_pairs={{0,48},{1,49},{16,0},{17,1},{32,16},{33,17},{48,32},{49,33},{64,11... | collective-permute-start | bytes 786440 | tf_op jit(solution)/shard_map/ppermute | solution.py:24
  52.2 4.5 %collective-permute-start.29 = (bf16[256,512]{1,0:T(8,128)(2,1)S(1)}, bf16[256,512]{1,0:T(8,128)(2,1)S(1)}, u32[]{:S(2)}, u32[]{:S(2)}) collective-permute-start(bf16[256,512]{1,0:T(8,128)(2,1)S(1)} %collective-permute-done.28.refs_6_), channel_id=1, source_target_pairs={{0,16},{1,17},{16,32},{17,33},{32,48},{33,49},{48,0},{49,1},{64,80... | collective-permute-start | bytes 786440 | tf_op jit(solution)/shard_map/ppermute | solution.py:24
  60.2 2.8 %collective-permute-done.29.refs_7_ = bf16[256,512]{1,0:T(8,128)(2,1)S(1)} collective-permute-done((bf16[256,512]{1,0:T(8,128)(2,1)S(1)}, bf16[256,512]{1,0:T(8,128)(2,1)S(1)}, u32[]{:S(2)}, u32[]{:S(2)}) %collective-permute-start.29) | collective-permute-done | bytes 262176 | tf_op jit(solution)/shard_map/ppermute | solution.py:24
  63.8 10.0 %first.3 = f32[8,256,512]{2,1,0:T(8,128)} custom-call(s32[32]{0:T(128)} %pad_add_fusion.meta, bf16[2048,1024]{1,0:T(8,128)(2,1)} %refs_1_.3, bf16[2048,1024]{1,0:T(8,128)(2,1)} %refs_1_.3, bf16[2048,1024]{1,0:T(8,128)(2,1)} %collective-permute-done.1.refs_2_.refs_3_, bf16[2048,1024]{1,0:T(8,128)(2,1)} %collective-permute-done.1.refs_2_.refs_3_, ...), custom_call_target="tpu_custom_call" | custom-call | flops 4294967296 | bytes 14680064 | tf_op jit(solution)/shard_map/first/pallas_call | solution.py:98
  76.3 5.9 %collective-permute-start.34 = (f16[256,512]{1,0:T(8,128)(2,1)S(1)}, f16[256,512]{1,0:T(8,128)(2,1)S(1)}, u32[]{:S(2)}, u32[]{:S(2)}) collective-permute-start(f16[256,512]{1,0:T(8,128)(2,1)S(1)} %get-tuple-element.13), channel_id=1, source_target_pairs={{0,12},{1,13},{16,28},{17,29},{32,44},{33,45},{48,60},{49,61},{64,... | collective-permute-start | bytes 786440 | tf_op jit(solution)/shard_map/ppermute | solution.py:24
  84.4 3.2 %collective-permute-start.8 = (bf16[256,256]{1,0:T(8,128)(2,1)S(1)}, bf16[256,256]{1,0:T(8,128)(2,1)S(1)}, u32[]{:S(2)}, u32[]{:S(2)}) collective-permute-start(bf16[256,256]{1,0:T(8,128)(2,1)S(1)} %collective-permute-done.7.refs_8_), channel_id=1, source_target_pairs={{0,48},{1,49},{16,0},{17,1},{32,16},{33,17},{48,32},{49,33},{64,11... | collective-permute-start | bytes 393224 | tf_op jit(solution)/shard_map/ppermute | solution.py:24
  87.6 2.9 %collective-permute-done.5.refs_6_ = bf16[256,256]{1,0:T(8,128)(2,1)S(1)} collective-permute-done((bf16[256,256]{1,0:T(8,128)(2,1)S(1)}, bf16[256,256]{1,0:T(8,128)(2,1)S(1)}, u32[]{:S(2)}, u32[]{:S(2)}) %collective-permute-start.5) | collective-permute-done | bytes 131104 | tf_op jit(solution)/shard_map/ppermute | solution.py:24
  93.1 3.5 %collective-permute-start.36 = (f16[256,512]{1,0:T(8,128)(2,1)S(1)}, f16[256,512]{1,0:T(8,128)(2,1)S(1)}, u32[]{:S(2)}, u32[]{:S(2)}) collective-permute-start(f16[256,512]{1,0:T(8,128)(2,1)S(1)} %get-tuple-element.18), channel_id=1, source_target_pairs={{0,14},{1,15},{16,30},{17,31},{32,46},{33,47},{48,62},{49,63},{64,... | collective-permute-start | bytes 786440 | tf_op jit(solution)/shard_map/ppermute | solution.py:24
  102.2 5.2 %collective-permute-done.37 = f16[256,512]{1,0:T(8,128)(2,1)S(1)} collective-permute-done((f16[256,512]{1,0:T(8,128)(2,1)S(1)}, f16[256,512]{1,0:T(8,128)(2,1)S(1)}, u32[]{:S(2)}, u32[]{:S(2)}) %collective-permute-start.37) | collective-permute-done | bytes 262176 | tf_op jit(solution)/shard_map/ppermute | solution.py:24
  107.5 3.2 %collective-permute-start.10 = (bf16[256,256]{1,0:T(8,128)(2,1)S(1)}, bf16[256,256]{1,0:T(8,128)(2,1)S(1)}, u32[]{:S(2)}, u32[]{:S(2)}) collective-permute-start(bf16[256,256]{1,0:T(8,128)(2,1)S(1)} %collective-permute-done.8.refs_9_), channel_id=1, source_target_pairs={{0,48},{1,49},{16,0},{17,1},{32,16},{33,17},{48,32},{49,33},{64,11... | collective-permute-start | bytes 393224 | tf_op jit(solution)/shard_map/ppermute | solution.py:24
  115.0 7.7 %first.2 = f32[8,256,256]{2,1,0:T(8,128)} custom-call(s32[32]{0:T(128)} %pad_add_fusion.meta, bf16[2048,1024]{1,0:T(8,128)(2,1)} %refs_1_.3, bf16[2048,1024]{1,0:T(8,128)(2,1)} %refs_1_.3, bf16[2048,1024]{1,0:T(8,128)(2,1)} %collective-permute-done.1.refs_2_.refs_3_, bf16[2048,1024]{1,0:T(8,128)(2,1)} %collective-permute-done.1.refs_2_.refs_3_, ...), custom_call_target="tpu_custom_call" | custom-call | flops 2147483648 | bytes 11534336 | tf_op jit(solution)/shard_map/first/pallas_call | solution.py:98
  122.7 2.8 %collective-permute-start.42 = (bf16[256,512]{1,0:T(8,128)(2,1)S(1)}, bf16[256,512]{1,0:T(8,128)(2,1)S(1)}, u32[]{:S(2)}, u32[]{:S(2)}) collective-permute-start(bf16[256,512]{1,0:T(8,128)(2,1)S(1)} %fusion.9.refs_0_), channel_id=1, source_target_pairs={{0,2},{1,3},{16,18},{17,19},{32,34},{33,35},{48,50},{49,51},{64,66... | collective-permute-start | bytes 786440 | tf_op jit(solution)/shard_map/ppermute | solution.py:24
  140.8 6.0 %collective-permute-done.17 = f16[256,256]{1,0:T(8,128)(2,1)S(1)} collective-permute-done((f16[256,256]{1,0:T(8,128)(2,1)S(1)}, f16[256,256]{1,0:T(8,128)(2,1)S(1)}, u32[]{:S(2)}, u32[]{:S(2)}) %collective-permute-start.17) | collective-permute-done | bytes 131104 | tf_op jit(solution)/shard_map/ppermute | solution.py:24
  151.2 2.7 %collective-permute-start.13 = (f16[256,256]{1,0:T(8,128)(2,1)}, f16[256,256]{1,0:T(8,128)(2,1)S(1)}, u32[]{:S(2)}, u32[]{:S(2)}) collective-permute-start(f16[256,256]{1,0:T(8,128)(2,1)} %get-tuple-element.25), channel_id=1, source_target_pairs={{0,14},{1,15},{16,30},{17,31},{32,46},{33,47},{48,62},{49,63},{64,... | collective-permute-start | bytes 393224 | tf_op jit(solution)/shard_map/ppermute | solution.py:24
  155.7 3.6 %order_rows.3.refs_1_ = bf16[2048,512]{1,0:T(8,128)(2,1)} custom-call(s32[32]{0:T(128)} %pad_add_fusion.meta, bf16[256,512]{1,0:T(8,128)(2,1)} %copy-done.4, bf16[256,512]{1,0:T(8,128)(2,1)} %copy-done.26, bf16[256,512]{1,0:T(8,128)(2,1)} %copy-done.24, bf16[256,512]{1,0:T(8,128)(2,1)} %copy-done.28, bf16[256,512]{1,0:T(8,128)(2,1)} %copy-done.23, ...), custom_call_target="tpu_custom_call" | custom-call | bytes 4194304 | tf_op jit(solution)/shard_map/order_rows/pallas_call | solution.py:127
  159.5 3.1 %collective-permute-done.12 = f16[256,256]{1,0:T(8,128)(2,1)S(1)} collective-permute-done((f16[256,256]{1,0:T(8,128)(2,1)S(1)}, f16[256,256]{1,0:T(8,128)(2,1)S(1)}, u32[]{:S(2)}, u32[]{:S(2)}) %collective-permute-start.12) | collective-permute-done | bytes 131104 | tf_op jit(solution)/shard_map/ppermute | solution.py:24
  165.3 2.7 %collective-permute-start.19 = (bf16[256,256]{1,0:T(8,128)(2,1)S(1)}, bf16[256,256]{1,0:T(8,128)(2,1)S(1)}, u32[]{:S(2)}, u32[]{:S(2)}) collective-permute-start(bf16[256,256]{1,0:T(8,128)(2,1)S(1)} %fusion.26.refs_0_), channel_id=1, source_target_pairs={{0,2},{1,3},{16,18},{17,19},{32,34},{33,35},{48,50},{49,51},{64,66... | collective-permute-start | bytes 393224 | tf_op jit(solution)/shard_map/ppermute | solution.py:24
  168.7 7.5 %collective-permute-start.18 = (bf16[256,256]{1,0:T(8,128)(2,1)S(1)}, bf16[256,256]{1,0:T(8,128)(2,1)S(1)}, u32[]{:S(2)}, u32[]{:S(2)}) collective-permute-start(bf16[256,256]{1,0:T(8,128)(2,1)S(1)} %fusion.26.refs_0_), channel_id=1, source_target_pairs={{0,6},{1,7},{16,22},{17,23},{32,38},{33,39},{48,54},{49,55},{64,70... | collective-permute-start | bytes 393224 | tf_op jit(solution)/shard_map/ppermute | solution.py:24
  192.3 3.0 %order_rows.2.refs_0_ = bf16[2048,256]{1,0:T(8,128)(2,1)} custom-call(s32[32]{0:T(128)} %pad_add_fusion.meta, bf16[256,256]{1,0:T(8,128)(2,1)} %copy-done.8, bf16[256,256]{1,0:T(8,128)(2,1)} %copy-done.46, bf16[256,256]{1,0:T(8,128)(2,1)} %copy-done.45, bf16[256,256]{1,0:T(8,128)(2,1)} %copy-done.48, bf16[256,256]{1,0:T(8,128)(2,1)} %copy-done.44, ...), custom_call_target="tpu_custom_call" | custom-call | bytes 2097152 | tf_op jit(solution)/shard_map/order_rows/pallas_call | solution.py:127
  195.3 2.8 %collective-permute-start.63 = (bf16[256,256]{1,0:T(8,128)(2,1)S(1)}, bf16[256,256]{1,0:T(8,128)(2,1)S(1)}, u32[]{:S(2)}, u32[]{:S(2)}) collective-permute-start(bf16[256,256]{1,0:T(8,128)(2,1)S(1)} %get-tuple-element.31.refs_12_), channel_id=1, source_target_pairs={{0,48},{1,49},{16,0},{17,1},{32,16},{33,17},{48,32},{49,33},{64,11... | collective-permute-start | bytes 393224 | tf_op jit(solution)/shard_map/ppermute | solution.py:24
  198.8 3.0 %collective-permute-start.58 = (bf16[256,512]{1,0:T(8,128)(2,1)S(1)}, bf16[256,512]{1,0:T(8,128)(2,1)S(1)}, u32[]{:S(2)}, u32[]{:S(2)}) collective-permute-start(bf16[256,512]{1,0:T(8,128)(2,1)S(1)} %collective-permute-done.57), channel_id=1, source_target_pairs={{0,64},{1,0},{16,80},{17,16},{32,96},{33,32},{48,112},{49,48},{64,... | collective-permute-start | bytes 786440 | tf_op jit(solution)/shard_map/ppermute | solution.py:24
  202.6 6.2 %collective-permute-done.54.refs_6_ = bf16[256,256]{1,0:T(8,128)(2,1)S(1)} collective-permute-done((bf16[256,256]{1,0:T(8,128)(2,1)S(1)}, bf16[256,256]{1,0:T(8,128)(2,1)S(1)}, u32[]{:S(2)}, u32[]{:S(2)}) %collective-permute-start.54) | collective-permute-done | bytes 131104 | tf_op jit(solution)/shard_map/ppermute | solution.py:24
  216.1 3.7 %collective-permute-start.67 = (bf16[256,512]{1,0:T(8,128)(2,1)S(1)}, bf16[256,512]{1,0:T(8,128)(2,1)S(1)}, u32[]{:S(2)}, u32[]{:S(2)}) collective-permute-start(bf16[256,512]{1,0:T(8,128)(2,1)S(1)} %get-tuple-element.29.refs_16_), channel_id=1, source_target_pairs={{0,48},{1,49},{16,0},{17,1},{32,16},{33,17},{48,32},{49,33},{64,11... | collective-permute-start | bytes 786440 | tf_op jit(solution)/shard_map/ppermute | solution.py:24
  219.8 5.2 %collective-permute-done.68.refs_18_ = bf16[256,512]{1,0:T(8,128)(2,1)S(1)} collective-permute-done((bf16[256,512]{1,0:T(8,128)(2,1)S(1)}, bf16[256,512]{1,0:T(8,128)(2,1)S(1)}, u32[]{:S(2)}, u32[]{:S(2)}) %collective-permute-start.68) | collective-permute-done | bytes 262176 | tf_op jit(solution)/shard_map/ppermute | solution.py:24
  226.9 2.7 %collective-permute-start.69 = (bf16[256,512]{1,0:T(8,128)(2,1)S(1)}, bf16[256,512]{1,0:T(8,128)(2,1)S(1)}, u32[]{:S(2)}, u32[]{:S(2)}) collective-permute-start(bf16[256,512]{1,0:T(8,128)(2,1)S(1)} %collective-permute-done.67.refs_17_), channel_id=1, source_target_pairs={{0,48},{1,49},{16,0},{17,1},{32,16},{33,17},{48,32},{49,33},{64,11... | collective-permute-start | bytes 786440 | tf_op jit(solution)/shard_map/ppermute | solution.py:24
  229.7 4.5 %collective-permute-done.59.refs_9_ = bf16[256,512]{1,0:T(8,128)(2,1)S(1)} collective-permute-done((bf16[256,512]{1,0:T(8,128)(2,1)S(1)}, bf16[256,512]{1,0:T(8,128)(2,1)S(1)}, u32[]{:S(2)}, u32[]{:S(2)}) %collective-permute-start.59) | collective-permute-done | bytes 262176 | tf_op jit(solution)/shard_map/ppermute | solution.py:24
  234.3 2.8 %collective-permute-done.69.refs_19_ = bf16[256,512]{1,0:T(8,128)(2,1)S(1)} collective-permute-done((bf16[256,512]{1,0:T(8,128)(2,1)S(1)}, bf16[256,512]{1,0:T(8,128)(2,1)S(1)}, u32[]{:S(2)}, u32[]{:S(2)}) %collective-permute-start.69) | collective-permute-done | bytes 262176 | tf_op jit(solution)/shard_map/ppermute | solution.py:24
  240.4 14.1 %second.1 = f32[2048,1024]{1,0:T(8,128)} custom-call(s32[32]{0:T(128)} %pad_add_fusion.meta, f32[2048,1024]{1,0:T(8,128)} %acc_ref.1, f32[2048,128]{1,0:T(8,128)} %broadcast_in_dim.71.gap_rows_ref, f32[1,1024]{1,0:T(1,128)} %bitcast.58, bf16[2048,256]{1,0:T(8,128)(2,1)} %order_rows.2.refs_0_, bf16[2048,512]{1,0:T(8,128)(2,1)} %order_rows.3.refs_1_, ...), custom_call_target="tpu_custom_call" | custom-call | flops 6442450944 | bytes 26214400 | tf_op jit(solution)/shard_map/second/pallas_call | solution.py:162
  (247 shorter events, 86.6 us)
Async XLA Ops:
  0.0 63.0 %collective-permute-start.1 = (bf16[2048,1024]{1,0:T(8,128)(2,1)}, bf16[2048,1024]{1,0:T(8,128)(2,1)}, u32[]{:S(2)}, u32[]{:S(2)}) collective-permute-start(bf16[2048,1024]{1,0:T(8,128)(2,1)} %refs_1_.3), channel_id=1, source_target_pairs={{0,1},{1,0},{16,17},{17,16},{32,33},{33,32},{48,49},{49,48},{64,65... | collective-permute-start | bytes 12582920 | tf_op jit(solution)/shard_map/ppermute | solution.py:24
  12.4 23.1 %collective-permute-start.30 = (bf16[256,512]{1,0:T(8,128)(2,1)S(1)}, bf16[256,512]{1,0:T(8,128)(2,1)S(1)}, u32[]{:S(2)}, u32[]{:S(2)}) collective-permute-start(bf16[256,512]{1,0:T(8,128)(2,1)S(1)} %collective-permute-done.26.refs_4_), channel_id=1, source_target_pairs={{0,64},{1,65},{16,80},{17,81},{32,96},{33,97},{48,112},{49,113},{6... | collective-permute-start | bytes 786440 | tf_op jit(solution)/shard_map/ppermute | solution.py:24
  22.6 20.8 %collective-permute-start.2 = (bf16[256,256]{1,0:T(8,128)(2,1)S(1)}, bf16[256,256]{1,0:T(8,128)(2,1)S(1)}, u32[]{:S(2)}, u32[]{:S(2)}) collective-permute-start(bf16[256,256]{1,0:T(8,128)(2,1)S(1)} %pad_maximum_fusion.1), channel_id=1, source_target_pairs={{0,0},{1,1},{16,16},{17,17},{32,32},{33,33},{48,48},{49,49},{64,64... | collective-permute-start | bytes 393224 | tf_op jit(solution)/shard_map/ppermute | solution.py:24
  24.1 28.0 %collective-permute-start.28 = (bf16[256,512]{1,0:T(8,128)(2,1)S(1)}, bf16[256,512]{1,0:T(8,128)(2,1)S(1)}, u32[]{:S(2)}, u32[]{:S(2)}) collective-permute-start(bf16[256,512]{1,0:T(8,128)(2,1)S(1)} %collective-permute-done.26.refs_4_), channel_id=1, source_target_pairs={{0,16},{1,17},{16,32},{17,33},{32,48},{33,49},{48,0},{49,1},{64,80... | collective-permute-start | bytes 786440 | tf_op jit(solution)/shard_map/ppermute | solution.py:24
  35.5 21.1 %collective-permute-start.31 = (bf16[256,512]{1,0:T(8,128)(2,1)S(1)}, bf16[256,512]{1,0:T(8,128)(2,1)S(1)}, u32[]{:S(2)}, u32[]{:S(2)}) collective-permute-start(bf16[256,512]{1,0:T(8,128)(2,1)S(1)} %collective-permute-done.30.refs_8_), channel_id=1, source_target_pairs={{0,48},{1,49},{16,0},{17,1},{32,16},{33,17},{48,32},{49,33},{64,11... | collective-permute-start | bytes 786440 | tf_op jit(solution)/shard_map/ppermute | solution.py:24
  44.1 14.5 %collective-permute-start.27 = (bf16[256,512]{1,0:T(8,128)(2,1)S(1)}, bf16[256,512]{1,0:T(8,128)(2,1)S(1)}, u32[]{:S(2)}, u32[]{:S(2)}) collective-permute-start(bf16[256,512]{1,0:T(8,128)(2,1)S(1)} %collective-permute-done.26.refs_4_), channel_id=1, source_target_pairs={{0,48},{1,49},{16,0},{17,1},{32,16},{33,17},{48,32},{49,33},{64,11... | collective-permute-start | bytes 786440 | tf_op jit(solution)/shard_map/ppermute | solution.py:24
  52.2 10.8 %collective-permute-start.29 = (bf16[256,512]{1,0:T(8,128)(2,1)S(1)}, bf16[256,512]{1,0:T(8,128)(2,1)S(1)}, u32[]{:S(2)}, u32[]{:S(2)}) collective-permute-start(bf16[256,512]{1,0:T(8,128)(2,1)S(1)} %collective-permute-done.28.refs_6_), channel_id=1, source_target_pairs={{0,16},{1,17},{16,32},{17,33},{32,48},{33,49},{48,0},{49,1},{64,80... | collective-permute-start | bytes 786440 | tf_op jit(solution)/shard_map/ppermute | solution.py:24
  58.6 25.8 %collective-permute-start.7 = (bf16[256,256]{1,0:T(8,128)(2,1)S(1)}, bf16[256,256]{1,0:T(8,128)(2,1)S(1)}, u32[]{:S(2)}, u32[]{:S(2)}) collective-permute-start(bf16[256,256]{1,0:T(8,128)(2,1)S(1)} %collective-permute-done.3.refs_4_), channel_id=1, source_target_pairs={{0,64},{1,65},{16,80},{17,81},{32,96},{33,97},{48,112},{49,113},{6... | collective-permute-start | bytes 393224 | tf_op jit(solution)/shard_map/ppermute | solution.py:24
  76.3 16.9 %collective-permute-start.34 = (f16[256,512]{1,0:T(8,128)(2,1)S(1)}, f16[256,512]{1,0:T(8,128)(2,1)S(1)}, u32[]{:S(2)}, u32[]{:S(2)}) collective-permute-start(f16[256,512]{1,0:T(8,128)(2,1)S(1)} %get-tuple-element.13), channel_id=1, source_target_pairs={{0,12},{1,13},{16,28},{17,29},{32,44},{33,45},{48,60},{49,61},{64,... | collective-permute-start | bytes 786440 | tf_op jit(solution)/shard_map/ppermute | solution.py:24
  82.2 14.9 %collective-permute-start.40 = (f16[256,512]{1,0:T(8,128)(2,1)S(1)}, f16[256,512]{1,0:T(8,128)(2,1)S(1)}, u32[]{:S(2)}, u32[]{:S(2)}) collective-permute-start(f16[256,512]{1,0:T(8,128)(2,1)S(1)} %get-tuple-element.14), channel_id=1, source_target_pairs={{0,6},{1,7},{16,22},{17,23},{32,38},{33,39},{48,54},{49,55},{64,70... | collective-permute-start | bytes 786440 | tf_op jit(solution)/shard_map/ppermute | solution.py:24
  87.6 12.6 %collective-permute-start.39 = (f16[256,512]{1,0:T(8,128)(2,1)S(1)}, f16[256,512]{1,0:T(8,128)(2,1)S(1)}, u32[]{:S(2)}, u32[]{:S(2)}) collective-permute-start(f16[256,512]{1,0:T(8,128)(2,1)S(1)} %get-tuple-element.15), channel_id=1, source_target_pairs={{0,2},{1,3},{16,18},{17,19},{32,34},{33,35},{48,50},{49,51},{64,66... | collective-permute-start | bytes 786440 | tf_op jit(solution)/shard_map/ppermute | solution.py:24
  92.5 15.0 %collective-permute-start.37 = (f16[256,512]{1,0:T(8,128)(2,1)S(1)}, f16[256,512]{1,0:T(8,128)(2,1)S(1)}, u32[]{:S(2)}, u32[]{:S(2)}) collective-permute-start(f16[256,512]{1,0:T(8,128)(2,1)S(1)} %get-tuple-element.17), channel_id=1, source_target_pairs={{0,8},{1,9},{16,24},{17,25},{32,40},{33,41},{48,56},{49,57},{64,72... | collective-permute-start | bytes 786440 | tf_op jit(solution)/shard_map/ppermute | solution.py:24
  93.1 14.3 %collective-permute-start.36 = (f16[256,512]{1,0:T(8,128)(2,1)S(1)}, f16[256,512]{1,0:T(8,128)(2,1)S(1)}, u32[]{:S(2)}, u32[]{:S(2)}) collective-permute-start(f16[256,512]{1,0:T(8,128)(2,1)S(1)} %get-tuple-element.18), channel_id=1, source_target_pairs={{0,14},{1,15},{16,30},{17,31},{32,46},{33,47},{48,62},{49,63},{64,... | collective-permute-start | bytes 786440 | tf_op jit(solution)/shard_map/ppermute | solution.py:24
  97.1 13.6 %collective-permute-start.35 = (f16[256,512]{1,0:T(8,128)(2,1)S(1)}, f16[256,512]{1,0:T(8,128)(2,1)S(1)}, u32[]{:S(2)}, u32[]{:S(2)}) collective-permute-start(f16[256,512]{1,0:T(8,128)(2,1)S(1)} %get-tuple-element.19), channel_id=1, source_target_pairs={{0,10},{1,11},{16,26},{17,27},{32,42},{33,43},{48,58},{49,59},{64,... | collective-permute-start | bytes 786440 | tf_op jit(solution)/shard_map/ppermute | solution.py:24
  100.2 12.2 %collective-permute-start.4 = (bf16[256,256]{1,0:T(8,128)(2,1)S(1)}, bf16[256,256]{1,0:T(8,128)(2,1)S(1)}, u32[]{:S(2)}, u32[]{:S(2)}) collective-permute-start(bf16[256,256]{1,0:T(8,128)(2,1)S(1)} %collective-permute-done.3.refs_4_), channel_id=1, source_target_pairs={{0,48},{1,49},{16,0},{17,1},{32,16},{33,17},{48,32},{49,33},{64,11... | collective-permute-start | bytes 393224 | tf_op jit(solution)/shard_map/ppermute | solution.py:24
  100.2 12.2 %collective-permute-start.9 = (bf16[256,256]{1,0:T(8,128)(2,1)S(1)}, bf16[256,256]{1,0:T(8,128)(2,1)S(1)}, u32[]{:S(2)}, u32[]{:S(2)}) collective-permute-start(bf16[256,256]{1,0:T(8,128)(2,1)S(1)} %collective-permute-done.7.refs_8_), channel_id=1, source_target_pairs={{0,16},{1,17},{16,32},{17,33},{32,48},{33,49},{48,0},{49,1},{64,80... | collective-permute-start | bytes 393224 | tf_op jit(solution)/shard_map/ppermute | solution.py:24
  112.1 13.4 %collective-permute-start.44 = (bf16[256,512]{1,0:T(8,128)(2,1)S(1)}, bf16[256,512]{1,0:T(8,128)(2,1)S(1)}, u32[]{:S(2)}, u32[]{:S(2)}) collective-permute-start(bf16[256,512]{1,0:T(8,128)(2,1)S(1)} %fusion.9.refs_0_), channel_id=1, source_target_pairs={{0,8},{1,9},{16,24},{17,25},{32,40},{33,41},{48,56},{49,57},{64,72... | collective-permute-start | bytes 786440 | tf_op jit(solution)/shard_map/ppermute | solution.py:24
  130.8 16.5 %collective-permute-start.41 = (bf16[256,512]{1,0:T(8,128)(2,1)S(1)}, bf16[256,512]{1,0:T(8,128)(2,1)S(1)}, u32[]{:S(2)}, u32[]{:S(2)}) collective-permute-start(bf16[256,512]{1,0:T(8,128)(2,1)S(1)} %fusion.9.refs_0_), channel_id=1, source_target_pairs={{0,6},{1,7},{16,22},{17,23},{32,38},{33,39},{48,54},{49,55},{64,70... | collective-permute-start | bytes 786440 | tf_op jit(solution)/shard_map/ppermute | solution.py:24
  133.1 16.8 %collective-permute-start.46 = (bf16[256,512]{1,0:T(8,128)(2,1)S(1)}, bf16[256,512]{1,0:T(8,128)(2,1)S(1)}, u32[]{:S(2)}, u32[]{:S(2)}) collective-permute-start(bf16[256,512]{1,0:T(8,128)(2,1)S(1)} %collective-permute-done.44.refs_4_), channel_id=1, source_target_pairs={{0,2},{1,3},{16,18},{17,19},{32,34},{33,35},{48,50},{49,51},{64,66... | collective-permute-start | bytes 786440 | tf_op jit(solution)/shard_map/ppermute | solution.py:24
  133.2 18.1 %collective-permute-start.43 = (bf16[256,512]{1,0:T(8,128)(2,1)S(1)}, bf16[256,512]{1,0:T(8,128)(2,1)S(1)}, u32[]{:S(2)}, u32[]{:S(2)}) collective-permute-start(bf16[256,512]{1,0:T(8,128)(2,1)S(1)} %collective-permute-done.42.refs_2_), channel_id=1, source_target_pairs={{0,2},{1,3},{16,18},{17,19},{32,34},{33,35},{48,50},{49,51},{64,66... | collective-permute-start | bytes 786440 | tf_op jit(solution)/shard_map/ppermute | solution.py:24
  134.6 19.3 %collective-permute-start.47 = (bf16[256,512]{1,0:T(8,128)(2,1)S(1)}, bf16[256,512]{1,0:T(8,128)(2,1)S(1)}, u32[]{:S(2)}, u32[]{:S(2)}) collective-permute-start(bf16[256,512]{1,0:T(8,128)(2,1)S(1)} %collective-permute-done.45.refs_5_), channel_id=1, source_target_pairs={{0,6},{1,7},{16,22},{17,23},{32,38},{33,39},{48,54},{49,55},{64,70... | collective-permute-start | bytes 786440 | tf_op jit(solution)/shard_map/ppermute | solution.py:24
  146.8 12.5 %collective-permute-start.16 = (f16[256,256]{1,0:T(8,128)(2,1)S(1)}, f16[256,256]{1,0:T(8,128)(2,1)S(1)}, u32[]{:S(2)}, u32[]{:S(2)}) collective-permute-start(f16[256,256]{1,0:T(8,128)(2,1)S(1)} %get-tuple-element.22), channel_id=1, source_target_pairs={{0,2},{1,3},{16,18},{17,19},{32,34},{33,35},{48,50},{49,51},{64,66... | collective-permute-start | bytes 393224 | tf_op jit(solution)/shard_map/ppermute | solution.py:24
  147.4 12.0 %collective-permute-start.15 = (f16[256,256]{1,0:T(8,128)(2,1)}, f16[256,256]{1,0:T(8,128)(2,1)S(1)}, u32[]{:S(2)}, u32[]{:S(2)}) collective-permute-start(f16[256,256]{1,0:T(8,128)(2,1)} %get-tuple-element.23), channel_id=1, source_target_pairs={{0,4},{1,5},{16,20},{17,21},{32,36},{33,37},{48,52},{49,53},{64,68... | collective-permute-start | bytes 393224 | tf_op jit(solution)/shard_map/ppermute | solution.py:24
  159.3 79.7 %collective-permute-start.49 = (bf16[2048,512]{1,0:T(8,128)(2,1)}, bf16[2048,512]{1,0:T(8,128)(2,1)S(1)}, u32[]{:S(2)}, u32[]{:S(2)}) collective-permute-start(bf16[2048,512]{1,0:T(8,128)(2,1)} %order_rows.3.refs_1_), channel_id=1, source_target_pairs={{0,1},{1,0},{16,17},{17,16},{32,33},{33,32},{48,49},{49,48},{64,65... | collective-permute-start | bytes 6291464 | tf_op jit(solution)/shard_map/ppermute | solution.py:24
  164.3 11.9 %collective-permute-start.21 = (bf16[256,256]{1,0:T(8,128)(2,1)S(1)}, bf16[256,256]{1,0:T(8,128)(2,1)S(1)}, u32[]{:S(2)}, u32[]{:S(2)}) collective-permute-start(bf16[256,256]{1,0:T(8,128)(2,1)S(1)} %fusion.26.refs_0_), channel_id=1, source_target_pairs={{0,8},{1,9},{16,24},{17,25},{32,40},{33,41},{48,56},{49,57},{64,72... | collective-permute-start | bytes 393224 | tf_op jit(solution)/shard_map/ppermute | solution.py:24
  165.3 12.3 %collective-permute-start.19 = (bf16[256,256]{1,0:T(8,128)(2,1)S(1)}, bf16[256,256]{1,0:T(8,128)(2,1)S(1)}, u32[]{:S(2)}, u32[]{:S(2)}) collective-permute-start(bf16[256,256]{1,0:T(8,128)(2,1)S(1)} %fusion.26.refs_0_), channel_id=1, source_target_pairs={{0,2},{1,3},{16,18},{17,19},{32,34},{33,35},{48,50},{49,51},{64,66... | collective-permute-start | bytes 393224 | tf_op jit(solution)/shard_map/ppermute | solution.py:24
  168.7 11.2 %collective-permute-start.18 = (bf16[256,256]{1,0:T(8,128)(2,1)S(1)}, bf16[256,256]{1,0:T(8,128)(2,1)S(1)}, u32[]{:S(2)}, u32[]{:S(2)}) collective-permute-start(bf16[256,256]{1,0:T(8,128)(2,1)S(1)} %fusion.26.refs_0_), channel_id=1, source_target_pairs={{0,6},{1,7},{16,22},{17,23},{32,38},{33,39},{48,54},{49,55},{64,70... | collective-permute-start | bytes 393224 | tf_op jit(solution)/shard_map/ppermute | solution.py:24
  176.2 10.9 %collective-permute-start.56 = (bf16[256,512]{1,0:T(8,128)(2,1)S(1)}, bf16[256,512]{1,0:T(8,128)(2,1)}, u32[]{:S(2)}, u32[]{:S(2)}) collective-permute-start(bf16[256,512]{1,0:T(8,128)(2,1)S(1)} %copy-done.5), channel_id=1, source_target_pairs={{0,0},{1,1},{16,16},{17,17},{32,32},{33,33},{48,48},{49,49},{64,64... | collective-permute-start | bytes 786440 | tf_op jit(solution)/shard_map/ppermute | solution.py:24
  187.1 11.0 %collective-permute-start.57 = (bf16[256,512]{1,0:T(8,128)(2,1)}, bf16[256,512]{1,0:T(8,128)(2,1)S(1)}, u32[]{:S(2)}, u32[]{:S(2)}) collective-permute-start(bf16[256,512]{1,0:T(8,128)(2,1)} %collective-permute-done.56), channel_id=1, source_target_pairs={{0,0},{1,1},{16,18},{17,19},{32,36},{33,37},{48,54},{49,55},{64,8}... | collective-permute-start | bytes 786440 | tf_op jit(solution)/shard_map/ppermute | solution.py:24
  195.3 39.0 %collective-permute-start.48 = (bf16[2048,256]{1,0:T(8,128)(2,1)}, bf16[2048,256]{1,0:T(8,128)(2,1)S(1)}, u32[]{:S(2)}, u32[]{:S(2)}) collective-permute-start(bf16[2048,256]{1,0:T(8,128)(2,1)} %order_rows.2.refs_0_), channel_id=1, source_target_pairs={{0,1},{1,0},{16,17},{17,16},{32,33},{33,32},{48,49},{49,48},{64,65... | collective-permute-start | bytes 3145736 | tf_op jit(solution)/shard_map/ppermute | solution.py:24
  198.1 12.8 %collective-permute-start.66 = (bf16[256,512]{1,0:T(8,128)(2,1)S(1)}, bf16[256,512]{1,0:T(8,128)(2,1)S(1)}, u32[]{:S(2)}, u32[]{:S(2)}) collective-permute-start(bf16[256,512]{1,0:T(8,128)(2,1)S(1)} %collective-permute-done.57), channel_id=1, source_target_pairs={{1,64},{17,80},{33,96},{49,112},{64,1},{80,17},{96,33},{112,49},{9... | collective-permute-start | bytes 786440 | tf_op jit(solution)/shard_map/ppermute | solution.py:24
  198.8 12.2 %collective-permute-start.58 = (bf16[256,512]{1,0:T(8,128)(2,1)S(1)}, bf16[256,512]{1,0:T(8,128)(2,1)S(1)}, u32[]{:S(2)}, u32[]{:S(2)}) collective-permute-start(bf16[256,512]{1,0:T(8,128)(2,1)S(1)} %collective-permute-done.57), channel_id=1, source_target_pairs={{0,64},{1,0},{16,80},{17,16},{32,96},{33,32},{48,112},{49,48},{64,... | collective-permute-start | bytes 786440 | tf_op jit(solution)/shard_map/ppermute | solution.py:24
  (93 other events, 1258.4 us)

commit v2 on v1

--- a/solution.py
+++ b/solution.py
@@ -9,7 +9,7 @@
 
 
 WIDTHS = (256, 512)
-ORDER = "SsRrYyQq*FfPpXUxONuZWnowzGVvgEe"
+ORDER = "SsRrYQ*yFqP+fMpmXUxONuZWnowzGVvgEe"
 SCALE = 64.0
 
 PLACES = [(x, h, l, z, c) for x in range(4) for h in range(2) for l in range(2) for z in range(4) for c in range(2)]
@@ -110,6 +110,7 @@
             bytes_accessed=8 * rows * (4 * depth + 6 * width),
             transcendentals=0,
         ),
+        compiler_params=pltpu.CompilerParams(vmem_limit_bytes=20 << 20),
         name="first",
     )(meta, own, own, other, other, *pieces)
 
@@ -131,6 +132,7 @@
             num_scalar_prefetch=1, grid=(), in_specs=[spec] * 8, out_specs=spec
         ),
         cost_estimate=pl.CostEstimate(flops=0, bytes_accessed=32 * rows * width, transcendentals=0),
+        compiler_params=pltpu.CompilerParams(vmem_limit_bytes=12 << 20),
         name="order_rows",
     )(meta, *pieces)
 
@@ -180,6 +182,7 @@
             bytes_accessed=rows * cols * 8 + 2 * (rows + cols) * depth,
             transcendentals=0,
         ),
+        compiler_params=pltpu.CompilerParams(vmem_limit_bytes=32 << 20),
         name="second",
     )(meta, accumulated, gap_rows, gap_cols, *row_parts, *col_parts)
 
@@ -225,7 +228,10 @@
 
     def P(self):
         self.partials = first_product(self.env.meta, self.env.own, self.env.other, self.b_pieces)
-        self.arrived = [send(narrow(self.partials[i]), along_col(*TARGETS[i])) for i in range(7)]
+        self.narrowed = [narrow(self.partials[i]) for i in range(7)]
+
+    def M(self):
+        self.arrived = [send(self.narrowed[i], along_col(*TARGETS[i])) for i in range(7)]
 
     def X(self):
         total = self.partials[7] + sum(widen(a) for a in self.arrived)
@@ -309,6 +315,9 @@
     for stage in ORDER:
         if stage == "*":
             env.other = send(amplitudes, other_core)
+        elif stage == "+":
+            tied = (chunks[0].narrowed, chunks[1].near, chunks[1].near_swapped)
+            chunks[0].narrowed, chunks[1].near, chunks[1].near_swapped = lax.optimization_barrier(tied)
         else:
             getattr(chunks[int(stage.islower())], stage.upper())()
     return second_product(

time: 257 us -> 249 us (0.969)
  waiting for transfers between devices: 55.3 us -> 79.5 us
  Pallas kernels: 38.4 us -> 24.5 us
  starting transfers between devices: 138 us -> 126 us
  other arithmetic: 13 us -> 5.87 us
    ppermute x70, waiting for transfers between devices: 55.3 us -> 79.5 us  [send(): return lax.ppermute(value, ('row', 'col'), pairs)]
    ppermute x70, starting transfers between devices: 138 us -> 126 us  [send(): return lax.ppermute(value, ('row', 'col'), pairs)]
    pallas_call x2, Pallas kernels: 6.61 us -> 1.29 us  [order_rows(): pl.pallas_call(order_rows_kernel, out_shape=jax.ShapeDtypeStruct((8 * row...]
    pallas_call x2, Pallas kernels: 17.7 us -> 12.4 us  [first_product(): pl.pallas_call(first_kernel, out_shape=jax.ShapeDtypeStruct((8, rows, wid...]
    convert_element_type x2, other arithmetic: 4.83 us -> 0.76 us  [narrow(): return (value * SCALE).astype(jnp.float16)]
    pallas_call x1, Pallas kernels: 14.1 us -> 10.8 us  [second_product(): pl.pallas_call(functools.partial(second_kernel, widths), out_shape=jax.Sh...]
    unnamed x110 -> x18, local copies, waits for them, and re-layouts: 5.51 us -> 5.6 us
  transfers between devices with their start and end apart: 70 -> 70, of which waited for: 24 -> 26; matrix products, arithmetic and copies ran while one was open for 7% -> 4% of each run, Pallas kernels for 10% -> 3%
where the time goes in v2:
time: 249 us; the launch traced here: 246 us
  starting transfers between devices  126 us (51%)
  waiting for transfers between devices  79.5 us (32%)
  Pallas kernels  24.5 us (10%)
  local copies, waits for them, and re-layouts  9.69 us (4%)
  other arithmetic  5.87 us (2%)
    ppermute x70, starting transfers between devices, send(): return lax.ppermute(value, ('row', 'col'), pairs)  126 us
    ppermute x70, waiting for transfers between devices, send(): return lax.ppermute(value, ('row', 'col'), pairs)  79.5 us
    pallas_call x2, Pallas kernels, first_product(): pl.pallas_call(first_kernel, out_shape=jax.ShapeDtypeStruct((8, rows, wid...  12.4 us
    pallas_call x1, Pallas kernels, second_product(): pl.pallas_call(functools.partial(second_kernel, widths), out_shape=jax.Sh...  10.8 us
    unnamed x18, local copies, waits for them, and re-layouts  5.6 us
  transfers between devices with their start and end apart: 70, of which 26 were waited for; matrix products, arithmetic and copies ran while one was open for 4% of the time, Pallas kernels for 3%

profile of v2, /device:TPU:0, one launch (start us, length us, event | category | flops | bytes accessed | tf_op | source)
XLA Modules:
  0.0 245.8 jit_solution(1381848622691155091)
XLA Ops:
  1.7 6.0 %collective-permute-done = bf16[128,768]{1,0:T(8,128)(2,1)S(1)} collective-permute-done((bf16[128,768]{1,0:T(8,128)(2,1)S(1)}, bf16[128,768]{1,0:T(8,128)(2,1)S(1)}, u32[]{:S(2)}, u32[]{:S(2)}) %collective-permute-start) | collective-permute-done | bytes 196640 | tf_op jit(solution)/shard_map/ppermute | solution.py:24
  12.4 8.4 %collective-permute-start.7 = (bf16[256,256]{1,0:T(8,128)(2,1)S(1)}, bf16[256,256]{1,0:T(8,128)(2,1)S(1)}, u32[]{:S(2)}, u32[]{:S(2)}) collective-permute-start(bf16[256,256]{1,0:T(8,128)(2,1)S(1)} %collective-permute-done.3.refs_4_), channel_id=1, source_target_pairs={{0,64},{1,65},{16,80},{17,81},{32,96},{33,97},{48,112},{49,113},{6... | collective-permute-start | bytes 393224 | tf_op jit(solution)/shard_map/ppermute | solution.py:24
  22.2 11.1 %collective-permute-start.5 = (bf16[256,256]{1,0:T(8,128)(2,1)S(1)}, bf16[256,256]{1,0:T(8,128)(2,1)S(1)}, u32[]{:S(2)}, u32[]{:S(2)}) collective-permute-start(bf16[256,256]{1,0:T(8,128)(2,1)S(1)} %collective-permute-done.3.refs_4_), channel_id=1, source_target_pairs={{0,16},{1,17},{16,32},{17,33},{32,48},{33,49},{48,0},{49,1},{64,80... | collective-permute-start | bytes 393224 | tf_op jit(solution)/shard_map/ppermute | solution.py:24
  33.3 5.2 %collective-permute-start.4 = (bf16[256,256]{1,0:T(8,128)(2,1)S(1)}, bf16[256,256]{1,0:T(8,128)(2,1)S(1)}, u32[]{:S(2)}, u32[]{:S(2)}) collective-permute-start(bf16[256,256]{1,0:T(8,128)(2,1)S(1)} %collective-permute-done.3.refs_4_), channel_id=1, source_target_pairs={{0,48},{1,49},{16,0},{17,1},{32,16},{33,17},{48,32},{49,33},{64,11... | collective-permute-start | bytes 393224 | tf_op jit(solution)/shard_map/ppermute | solution.py:24
  48.6 2.7 %collective-permute-done.9.refs_10_ = bf16[256,256]{1,0:T(8,128)(2,1)S(1)} collective-permute-done((bf16[256,256]{1,0:T(8,128)(2,1)S(1)}, bf16[256,256]{1,0:T(8,128)(2,1)S(1)}, u32[]{:S(2)}, u32[]{:S(2)}) %collective-permute-start.9) | collective-permute-done | bytes 131104 | tf_op jit(solution)/shard_map/ppermute | solution.py:24
  51.4 2.8 %collective-permute-done.6.refs_7_ = bf16[256,256]{1,0:T(8,128)(2,1)S(1)} collective-permute-done((bf16[256,256]{1,0:T(8,128)(2,1)S(1)}, bf16[256,256]{1,0:T(8,128)(2,1)S(1)}, u32[]{:S(2)}, u32[]{:S(2)}) %collective-permute-start.6) | collective-permute-done | bytes 131104 | tf_op jit(solution)/shard_map/ppermute | solution.py:24
  60.0 5.3 %first.2 = f32[8,256,256]{2,1,0:T(8,128)S(1)} custom-call(s32[32]{0:T(128)S(1)} %pad_add_fusion.meta, bf16[2048,1024]{1,0:T(8,128)(2,1)S(1)} %copy-done, bf16[2048,1024]{1,0:T(8,128)(2,1)S(1)} %copy-done, bf16[2048,1024]{1,0:T(8,128)(2,1)} %collective-permute-done.1.refs_2_.refs_3_, bf16[2048,1024]{1,0:T(8,128)(2,1)} %collective-permute-done.1.refs_2_.refs_3_, ...), custom_call_target="tpu_custom_call" | custom-call | flops 2147483648 | bytes 11534336 | tf_op jit(solution)/shard_map/first/pallas_call | solution.py:98
  66.2 3.2 %collective-permute-start.33 = (bf16[256,512]{1,0:T(8,128)(2,1)S(1)}, bf16[256,512]{1,0:T(8,128)(2,1)S(1)}, u32[]{:S(2)}, u32[]{:S(2)}) collective-permute-start(bf16[256,512]{1,0:T(8,128)(2,1)S(1)} %collective-permute-done.16.refs_9_), channel_id=1, source_target_pairs={{0,48},{1,49},{16,0},{17,1},{32,16},{33,17},{48,32},{49,33},{64,11... | collective-permute-start | bytes 786440 | tf_op jit(solution)/shard_map/ppermute | solution.py:24
  69.4 4.3 %collective-permute-done.32.refs_7_ = bf16[256,512]{1,0:T(8,128)(2,1)S(1)} collective-permute-done((bf16[256,512]{1,0:T(8,128)(2,1)S(1)}, bf16[256,512]{1,0:T(8,128)(2,1)S(1)}, u32[]{:S(2)}, u32[]{:S(2)}) %collective-permute-start.32) | collective-permute-done | bytes 262176 | tf_op jit(solution)/shard_map/ppermute | solution.py:24
  73.7 7.0 %first.3 = f32[8,256,512]{2,1,0:T(8,128)S(1)} custom-call(s32[32]{0:T(128)S(1)} %pad_add_fusion.meta, bf16[2048,1024]{1,0:T(8,128)(2,1)S(1)} %copy-done, bf16[2048,1024]{1,0:T(8,128)(2,1)S(1)} %copy-done, bf16[2048,1024]{1,0:T(8,128)(2,1)} %collective-permute-done.1.refs_2_.refs_3_, bf16[2048,1024]{1,0:T(8,128)(2,1)} %collective-permute-done.1.refs_2_.refs_3_, ...), custom_call_target="tpu_custom_call" | custom-call | flops 4294967296 | bytes 14680064 | tf_op jit(solution)/shard_map/first/pallas_call | solution.py:98
  81.3 2.9 %collective-permute-start.34 = (f16[256,512]{1,0:T(8,128)(2,1)S(1)}, f16[256,512]{1,0:T(8,128)(2,1)S(1)}, u32[]{:S(2)}, u32[]{:S(2)}) collective-permute-start(f16[256,512]{1,0:T(8,128)(2,1)S(1)} %get-tuple-element.35), channel_id=1, source_target_pairs={{0,12},{1,13},{16,28},{17,29},{32,44},{33,45},{48,60},{49,61},{64,... | collective-permute-start | bytes 786440 | tf_op jit(solution)/shard_map/ppermute | solution.py:24
  89.9 4.5 %collective-permute-done.34 = f16[256,512]{1,0:T(8,128)(2,1)S(1)} collective-permute-done((f16[256,512]{1,0:T(8,128)(2,1)S(1)}, f16[256,512]{1,0:T(8,128)(2,1)S(1)}, u32[]{:S(2)}, u32[]{:S(2)}) %collective-permute-start.34) | collective-permute-done | bytes 262176 | tf_op jit(solution)/shard_map/ppermute | solution.py:24
  94.4 4.2 %collective-permute-start.36 = (f16[256,512]{1,0:T(8,128)(2,1)S(1)}, f16[256,512]{1,0:T(8,128)(2,1)S(1)}, u32[]{:S(2)}, u32[]{:S(2)}) collective-permute-start(f16[256,512]{1,0:T(8,128)(2,1)S(1)} %get-tuple-element.40), channel_id=1, source_target_pairs={{0,14},{1,15},{16,30},{17,31},{32,46},{33,47},{48,62},{49,63},{64,... | collective-permute-start | bytes 786440 | tf_op jit(solution)/shard_map/ppermute | solution.py:24
  99.7 3.5 %collective-permute-done.36 = f16[256,512]{1,0:T(8,128)(2,1)S(1)} collective-permute-done((f16[256,512]{1,0:T(8,128)(2,1)S(1)}, f16[256,512]{1,0:T(8,128)(2,1)S(1)}, u32[]{:S(2)}, u32[]{:S(2)}) %collective-permute-start.36) | collective-permute-done | bytes 262176 | tf_op jit(solution)/shard_map/ppermute | solution.py:24
  103.2 7.8 %collective-permute-done.35 = f16[256,512]{1,0:T(8,128)(2,1)S(1)} collective-permute-done((f16[256,512]{1,0:T(8,128)(2,1)S(1)}, f16[256,512]{1,0:T(8,128)(2,1)S(1)}, u32[]{:S(2)}, u32[]{:S(2)}) %collective-permute-start.35) | collective-permute-done | bytes 262176 | tf_op jit(solution)/shard_map/ppermute | solution.py:24
  111.6 9.2 %collective-permute-done.44.refs_4_ = bf16[256,512]{1,0:T(8,128)(2,1)S(1)} collective-permute-done((bf16[256,512]{1,0:T(8,128)(2,1)S(1)}, bf16[256,512]{1,0:T(8,128)(2,1)S(1)}, u32[]{:S(2)}, u32[]{:S(2)}) %collective-permute-start.44) | collective-permute-done | bytes 262176 | tf_op jit(solution)/shard_map/ppermute | solution.py:24
  120.8 3.6 %collective-permute-start.41 = (bf16[256,512]{1,0:T(8,128)(2,1)S(1)}, bf16[256,512]{1,0:T(8,128)(2,1)S(1)}, u32[]{:S(2)}, u32[]{:S(2)}) collective-permute-start(bf16[256,512]{1,0:T(8,128)(2,1)S(1)} %fusion.9.refs_0_), channel_id=1, source_target_pairs={{0,6},{1,7},{16,22},{17,23},{32,38},{33,39},{48,54},{49,55},{64,70... | collective-permute-start | bytes 786440 | tf_op jit(solution)/shard_map/ppermute | solution.py:24
  130.7 11.7 %collective-permute-done.19 = f16[256,256]{1,0:T(8,128)(2,1)S(1)} collective-permute-done((f16[256,256]{1,0:T(8,128)(2,1)S(1)}, f16[256,256]{1,0:T(8,128)(2,1)S(1)}, u32[]{:S(2)}, u32[]{:S(2)}) %collective-permute-start.19) | collective-permute-done | bytes 131104 | tf_op jit(solution)/shard_map/ppermute | solution.py:24
  143.1 3.0 %collective-permute-start.22 = (f16[256,256]{1,0:T(8,128)(2,1)S(1)}, f16[256,256]{1,0:T(8,128)(2,1)S(1)}, u32[]{:S(2)}, u32[]{:S(2)}) collective-permute-start(f16[256,256]{1,0:T(8,128)(2,1)S(1)} %get-tuple-element.26), channel_id=1, source_target_pairs={{0,4},{1,5},{16,20},{17,21},{32,36},{33,37},{48,52},{49,53},{64,68... | collective-permute-start | bytes 393224 | tf_op jit(solution)/shard_map/ppermute | solution.py:24
  147.5 2.7 %collective-permute-start.24 = (f16[256,256]{1,0:T(8,128)(2,1)S(1)}, f16[256,256]{1,0:T(8,128)(2,1)S(1)}, u32[]{:S(2)}, u32[]{:S(2)}) collective-permute-start(f16[256,256]{1,0:T(8,128)(2,1)S(1)} %get-tuple-element.28), channel_id=1, source_target_pairs={{0,6},{1,7},{16,22},{17,23},{32,38},{33,39},{48,54},{49,55},{64,70... | collective-permute-start | bytes 393224 | tf_op jit(solution)/shard_map/ppermute | solution.py:24
  154.8 2.8 %collective-permute-start.26 = (bf16[256,256]{1,0:T(8,128)(2,1)S(1)}, bf16[256,256]{1,0:T(8,128)(2,1)S(1)}, u32[]{:S(2)}, u32[]{:S(2)}) collective-permute-start(bf16[256,256]{1,0:T(8,128)(2,1)S(1)} %fusion.26.refs_0_), channel_id=1, source_target_pairs={{0,2},{1,3},{16,18},{17,19},{32,34},{33,35},{48,50},{49,51},{64,66... | collective-permute-start | bytes 393224 | tf_op jit(solution)/shard_map/ppermute | solution.py:24
  160.5 7.8 %collective-permute-start.29 = (bf16[256,256]{1,0:T(8,128)(2,1)S(1)}, bf16[256,256]{1,0:T(8,128)(2,1)S(1)}, u32[]{:S(2)}, u32[]{:S(2)}) collective-permute-start(bf16[256,256]{1,0:T(8,128)(2,1)S(1)} %collective-permute-done.28.refs_4_), channel_id=1, source_target_pairs={{0,6},{1,7},{16,22},{17,23},{32,38},{33,39},{48,54},{49,55},{64,70... | collective-permute-start | bytes 393224 | tf_op jit(solution)/shard_map/ppermute | solution.py:24
  169.6 3.7 %collective-permute-start.27 = (bf16[256,256]{1,0:T(8,128)(2,1)S(1)}, bf16[256,256]{1,0:T(8,128)(2,1)S(1)}, u32[]{:S(2)}, u32[]{:S(2)}) collective-permute-start(bf16[256,256]{1,0:T(8,128)(2,1)S(1)} %collective-permute-done.26.refs_2_), channel_id=1, source_target_pairs={{0,2},{1,3},{16,18},{17,19},{32,34},{33,35},{48,50},{49,51},{64,66... | collective-permute-start | bytes 393224 | tf_op jit(solution)/shard_map/ppermute | solution.py:24
  184.7 8.5 %collective-permute-start.58 = (bf16[256,512]{1,0:T(8,128)(2,1)S(1)}, bf16[256,512]{1,0:T(8,128)(2,1)S(1)}, u32[]{:S(2)}, u32[]{:S(2)}) collective-permute-start(bf16[256,512]{1,0:T(8,128)(2,1)S(1)} %collective-permute-done.57), channel_id=1, source_target_pairs={{0,64},{1,0},{16,80},{17,16},{32,96},{33,32},{48,112},{49,48},{64,... | collective-permute-start | bytes 786440 | tf_op jit(solution)/shard_map/ppermute | solution.py:24
  193.2 4.3 %collective-permute-start.63 = (bf16[256,256]{1,0:T(8,128)(2,1)S(1)}, bf16[256,256]{1,0:T(8,128)(2,1)S(1)}, u32[]{:S(2)}, u32[]{:S(2)}) collective-permute-start(bf16[256,256]{1,0:T(8,128)(2,1)S(1)} %get-tuple-element.53.refs_12_), channel_id=1, source_target_pairs={{0,48},{1,49},{16,0},{17,1},{32,16},{33,17},{48,32},{49,33},{64,11... | collective-permute-start | bytes 393224 | tf_op jit(solution)/shard_map/ppermute | solution.py:24
  197.6 3.1 %collective-permute-done.63.refs_13_ = bf16[256,256]{1,0:T(8,128)(2,1)S(1)} collective-permute-done((bf16[256,256]{1,0:T(8,128)(2,1)S(1)}, bf16[256,256]{1,0:T(8,128)(2,1)S(1)}, u32[]{:S(2)}, u32[]{:S(2)}) %collective-permute-start.63) | collective-permute-done | bytes 131104 | tf_op jit(solution)/shard_map/ppermute | solution.py:24
  200.7 3.7 %collective-permute-start.53 = (bf16[256,256]{1,0:T(8,128)(2,1)S(1)}, bf16[256,256]{1,0:T(8,128)(2,1)S(1)}, u32[]{:S(2)}, u32[]{:S(2)}) collective-permute-start(bf16[256,256]{1,0:T(8,128)(2,1)S(1)} %get-tuple-element.54.refs_4_), channel_id=1, source_target_pairs={{0,48},{1,49},{16,0},{17,1},{32,16},{33,17},{48,32},{49,33},{64,11... | collective-permute-start | bytes 393224 | tf_op jit(solution)/shard_map/ppermute | solution.py:24
  213.0 6.5 %collective-permute-done.55.refs_7_ = bf16[256,256]{1,0:T(8,128)(2,1)S(1)} collective-permute-done((bf16[256,256]{1,0:T(8,128)(2,1)S(1)}, bf16[256,256]{1,0:T(8,128)(2,1)S(1)}, u32[]{:S(2)}, u32[]{:S(2)}) %collective-permute-start.55) | collective-permute-done | bytes 131104 | tf_op jit(solution)/shard_map/ppermute | solution.py:24
  219.5 3.2 %collective-permute-start.59 = (bf16[256,512]{1,0:T(8,128)(2,1)S(1)}, bf16[256,512]{1,0:T(8,128)(2,1)S(1)}, u32[]{:S(2)}, u32[]{:S(2)}) collective-permute-start(bf16[256,512]{1,0:T(8,128)(2,1)S(1)} %get-tuple-element.52.refs_8_), channel_id=1, source_target_pairs={{0,48},{1,49},{16,0},{17,1},{32,16},{33,17},{48,32},{49,33},{64,11... | collective-permute-start | bytes 786440 | tf_op jit(solution)/shard_map/ppermute | solution.py:24
  224.8 4.0 %collective-permute-done.68.refs_18_ = bf16[256,512]{1,0:T(8,128)(2,1)S(1)} collective-permute-done((bf16[256,512]{1,0:T(8,128)(2,1)S(1)}, bf16[256,512]{1,0:T(8,128)(2,1)S(1)}, u32[]{:S(2)}, u32[]{:S(2)}) %collective-permute-start.68) | collective-permute-done | bytes 262176 | tf_op jit(solution)/shard_map/ppermute | solution.py:24
  231.6 3.4 %copy-done.1 = f32[2048,1024]{1,0:T(8,128)S(1)} copy-done((f32[2048,1024]{1,0:T(8,128)S(1)}, f32[2048,1024]{1,0:T(8,128)}, u32[]{:S(2)}) %copy-start.1) | copy-done | bytes 8388632
  235.0 10.8 %second.1 = f32[2048,1024]{1,0:T(8,128)} custom-call(s32[32]{0:T(128)S(1)} %pad_add_fusion.meta, f32[2048,1024]{1,0:T(8,128)S(1)} %copy-done.1, f32[2048,128]{1,0:T(8,128)S(1)} %copy-done.2, f32[1,1024]{1,0:T(1,128)S(1)} %bitcast.58, bf16[2048,256]{1,0:T(8,128)(2,1)S(1)} %order_rows.2.refs_0_, bf16[2048,512]{1,0:T(8,128)(2,1)S(1)} %order_rows.3.refs_1_, ...), custom_call_target="tpu_custom_call" | custom-call | flops 6442450944 | bytes 26214400 | tf_op jit(solution)/shard_map/second/pallas_call | solution.py:164
  (155 shorter events, 74.2 us)
Async XLA Ops:
  0.0 57.8 %collective-permute-start.1 = (bf16[2048,1024]{1,0:T(8,128)(2,1)}, bf16[2048,1024]{1,0:T(8,128)(2,1)}, u32[]{:S(2)}, u32[]{:S(2)}) collective-permute-start(bf16[2048,1024]{1,0:T(8,128)(2,1)} %refs_1_.3), channel_id=1, source_target_pairs={{0,1},{1,0},{16,17},{17,16},{32,33},{33,32},{48,49},{49,48},{64,65... | collective-permute-start | bytes 12582920 | tf_op jit(solution)/shard_map/ppermute | solution.py:24
  9.5 11.3 %collective-permute-start.11 = (bf16[256,512]{1,0:T(8,128)(2,1)S(1)}, bf16[256,512]{1,0:T(8,128)(2,1)S(1)}, u32[]{:S(2)}, u32[]{:S(2)}) collective-permute-start(bf16[256,512]{1,0:T(8,128)(2,1)S(1)} %pad_maximum_fusion), channel_id=1, source_target_pairs={{0,0},{1,1},{16,16},{17,17},{32,32},{33,33},{48,48},{49,49},{64,64... | collective-permute-start | bytes 786440 | tf_op jit(solution)/shard_map/ppermute | solution.py:24
  12.4 26.1 %collective-permute-start.7 = (bf16[256,256]{1,0:T(8,128)(2,1)S(1)}, bf16[256,256]{1,0:T(8,128)(2,1)S(1)}, u32[]{:S(2)}, u32[]{:S(2)}) collective-permute-start(bf16[256,256]{1,0:T(8,128)(2,1)S(1)} %collective-permute-done.3.refs_4_), channel_id=1, source_target_pairs={{0,64},{1,65},{16,80},{17,81},{32,96},{33,97},{48,112},{49,113},{6... | collective-permute-start | bytes 393224 | tf_op jit(solution)/shard_map/ppermute | solution.py:24
  20.8 20.7 %collective-permute-start.12 = (bf16[256,512]{1,0:T(8,128)(2,1)S(1)}, bf16[256,512]{1,0:T(8,128)(2,1)S(1)}, u32[]{:S(2)}, u32[]{:S(2)}) collective-permute-start(bf16[256,512]{1,0:T(8,128)(2,1)S(1)} %collective-permute-done.11), channel_id=1, source_target_pairs={{0,0},{1,1},{16,18},{17,19},{32,36},{33,37},{48,54},{49,55},{64,8}... | collective-permute-start | bytes 786440 | tf_op jit(solution)/shard_map/ppermute | solution.py:24
  22.2 21.5 %collective-permute-start.5 = (bf16[256,256]{1,0:T(8,128)(2,1)S(1)}, bf16[256,256]{1,0:T(8,128)(2,1)S(1)}, u32[]{:S(2)}, u32[]{:S(2)}) collective-permute-start(bf16[256,256]{1,0:T(8,128)(2,1)S(1)} %collective-permute-done.3.refs_4_), channel_id=1, source_target_pairs={{0,16},{1,17},{16,32},{17,33},{32,48},{33,49},{48,0},{49,1},{64,80... | collective-permute-start | bytes 393224 | tf_op jit(solution)/shard_map/ppermute | solution.py:24
  41.5 13.1 %collective-permute-start.15 = (bf16[256,512]{1,0:T(8,128)(2,1)S(1)}, bf16[256,512]{1,0:T(8,128)(2,1)S(1)}, u32[]{:S(2)}, u32[]{:S(2)}) collective-permute-start(bf16[256,512]{1,0:T(8,128)(2,1)S(1)} %collective-permute-done.12.refs_4_), channel_id=1, source_target_pairs={{0,64},{1,65},{16,80},{17,81},{32,96},{33,97},{48,112},{49,113},{6... | collective-permute-start | bytes 786440 | tf_op jit(solution)/shard_map/ppermute | solution.py:24
  44.9 11.3 %collective-permute-start.10 = (bf16[256,256]{1,0:T(8,128)(2,1)S(1)}, bf16[256,256]{1,0:T(8,128)(2,1)S(1)}, u32[]{:S(2)}, u32[]{:S(2)}) collective-permute-start(bf16[256,256]{1,0:T(8,128)(2,1)S(1)} %collective-permute-done.8.refs_9_), channel_id=1, source_target_pairs={{0,48},{1,49},{16,0},{17,1},{32,16},{33,17},{48,32},{49,33},{64,11... | collective-permute-start | bytes 393224 | tf_op jit(solution)/shard_map/ppermute | solution.py:24
  51.4 14.2 %collective-permute-start.14 = (bf16[256,512]{1,0:T(8,128)(2,1)S(1)}, bf16[256,512]{1,0:T(8,128)(2,1)S(1)}, u32[]{:S(2)}, u32[]{:S(2)}) collective-permute-start(bf16[256,512]{1,0:T(8,128)(2,1)S(1)} %collective-permute-done.12.refs_4_), channel_id=1, source_target_pairs={{0,16},{1,17},{16,32},{17,33},{32,48},{33,49},{48,0},{49,1},{64,80... | collective-permute-start | bytes 786440 | tf_op jit(solution)/shard_map/ppermute | solution.py:24
  54.2 11.5 %collective-permute-start.13 = (bf16[256,512]{1,0:T(8,128)(2,1)S(1)}, bf16[256,512]{1,0:T(8,128)(2,1)S(1)}, u32[]{:S(2)}, u32[]{:S(2)}) collective-permute-start(bf16[256,512]{1,0:T(8,128)(2,1)S(1)} %collective-permute-done.12.refs_4_), channel_id=1, source_target_pairs={{0,48},{1,49},{16,0},{17,1},{32,16},{33,17},{48,32},{49,33},{64,11... | collective-permute-start | bytes 786440 | tf_op jit(solution)/shard_map/ppermute | solution.py:24
  54.6 11.0 %collective-permute-start.17 = (bf16[256,512]{1,0:T(8,128)(2,1)S(1)}, bf16[256,512]{1,0:T(8,128)(2,1)S(1)}, u32[]{:S(2)}, u32[]{:S(2)}) collective-permute-start(bf16[256,512]{1,0:T(8,128)(2,1)S(1)} %collective-permute-done.15.refs_8_), channel_id=1, source_target_pairs={{0,16},{1,17},{16,32},{17,33},{32,48},{33,49},{48,0},{49,1},{64,80... | collective-permute-start | bytes 786440 | tf_op jit(solution)/shard_map/ppermute | solution.py:24
  81.3 13.1 %collective-permute-start.34 = (f16[256,512]{1,0:T(8,128)(2,1)S(1)}, f16[256,512]{1,0:T(8,128)(2,1)S(1)}, u32[]{:S(2)}, u32[]{:S(2)}) collective-permute-start(f16[256,512]{1,0:T(8,128)(2,1)S(1)} %get-tuple-element.35), channel_id=1, source_target_pairs={{0,12},{1,13},{16,28},{17,29},{32,44},{33,45},{48,60},{49,61},{64,... | collective-permute-start | bytes 786440 | tf_op jit(solution)/shard_map/ppermute | solution.py:24
  84.3 14.4 %collective-permute-start.40 = (f16[256,512]{1,0:T(8,128)(2,1)S(1)}, f16[256,512]{1,0:T(8,128)(2,1)S(1)}, u32[]{:S(2)}, u32[]{:S(2)}) collective-permute-start(f16[256,512]{1,0:T(8,128)(2,1)S(1)} %get-tuple-element.36), channel_id=1, source_target_pairs={{0,6},{1,7},{16,22},{17,23},{32,38},{33,39},{48,54},{49,55},{64,70... | collective-permute-start | bytes 786440 | tf_op jit(solution)/shard_map/ppermute | solution.py:24
  84.3 15.2 %collective-permute-start.39 = (f16[256,512]{1,0:T(8,128)(2,1)S(1)}, f16[256,512]{1,0:T(8,128)(2,1)S(1)}, u32[]{:S(2)}, u32[]{:S(2)}) collective-permute-start(f16[256,512]{1,0:T(8,128)(2,1)S(1)} %get-tuple-element.37), channel_id=1, source_target_pairs={{0,2},{1,3},{16,18},{17,19},{32,34},{33,35},{48,50},{49,51},{64,66... | collective-permute-start | bytes 786440 | tf_op jit(solution)/shard_map/ppermute | solution.py:24
  86.3 13.2 %collective-permute-start.38 = (f16[256,512]{1,0:T(8,128)(2,1)S(1)}, f16[256,512]{1,0:T(8,128)(2,1)S(1)}, u32[]{:S(2)}, u32[]{:S(2)}) collective-permute-start(f16[256,512]{1,0:T(8,128)(2,1)S(1)} %get-tuple-element.38), channel_id=1, source_target_pairs={{0,4},{1,5},{16,20},{17,21},{32,36},{33,37},{48,52},{49,53},{64,68... | collective-permute-start | bytes 786440 | tf_op jit(solution)/shard_map/ppermute | solution.py:24
  88.7 11.1 %collective-permute-start.37 = (f16[256,512]{1,0:T(8,128)(2,1)S(1)}, f16[256,512]{1,0:T(8,128)(2,1)S(1)}, u32[]{:S(2)}, u32[]{:S(2)}) collective-permute-start(f16[256,512]{1,0:T(8,128)(2,1)S(1)} %get-tuple-element.39), channel_id=1, source_target_pairs={{0,8},{1,9},{16,24},{17,25},{32,40},{33,41},{48,56},{49,57},{64,72... | collective-permute-start | bytes 786440 | tf_op jit(solution)/shard_map/ppermute | solution.py:24
  98.7 12.4 %collective-permute-start.35 = (f16[256,512]{1,0:T(8,128)(2,1)S(1)}, f16[256,512]{1,0:T(8,128)(2,1)S(1)}, u32[]{:S(2)}, u32[]{:S(2)}) collective-permute-start(f16[256,512]{1,0:T(8,128)(2,1)S(1)} %get-tuple-element.41), channel_id=1, source_target_pairs={{0,10},{1,11},{16,26},{17,27},{32,42},{33,43},{48,58},{49,59},{64,... | collective-permute-start | bytes 786440 | tf_op jit(solution)/shard_map/ppermute | solution.py:24
  111.5 13.0 %collective-permute-start.42 = (bf16[256,512]{1,0:T(8,128)(2,1)S(1)}, bf16[256,512]{1,0:T(8,128)(2,1)S(1)}, u32[]{:S(2)}, u32[]{:S(2)}) collective-permute-start(bf16[256,512]{1,0:T(8,128)(2,1)S(1)} %fusion.9.refs_0_), channel_id=1, source_target_pairs={{0,2},{1,3},{16,18},{17,19},{32,34},{33,35},{48,50},{49,51},{64,66... | collective-permute-start | bytes 786440 | tf_op jit(solution)/shard_map/ppermute | solution.py:24
  120.8 21.6 %collective-permute-start.41 = (bf16[256,512]{1,0:T(8,128)(2,1)S(1)}, bf16[256,512]{1,0:T(8,128)(2,1)S(1)}, u32[]{:S(2)}, u32[]{:S(2)}) collective-permute-start(bf16[256,512]{1,0:T(8,128)(2,1)S(1)} %fusion.9.refs_0_), channel_id=1, source_target_pairs={{0,6},{1,7},{16,22},{17,23},{32,38},{33,39},{48,54},{49,55},{64,70... | collective-permute-start | bytes 786440 | tf_op jit(solution)/shard_map/ppermute | solution.py:24
  124.4 18.7 %collective-permute-start.46 = (bf16[256,512]{1,0:T(8,128)(2,1)S(1)}, bf16[256,512]{1,0:T(8,128)(2,1)S(1)}, u32[]{:S(2)}, u32[]{:S(2)}) collective-permute-start(bf16[256,512]{1,0:T(8,128)(2,1)S(1)} %collective-permute-done.44.refs_4_), channel_id=1, source_target_pairs={{0,2},{1,3},{16,18},{17,19},{32,34},{33,35},{48,50},{49,51},{64,66... | collective-permute-start | bytes 786440 | tf_op jit(solution)/shard_map/ppermute | solution.py:24
  124.4 21.7 %collective-permute-start.43 = (bf16[256,512]{1,0:T(8,128)(2,1)S(1)}, bf16[256,512]{1,0:T(8,128)(2,1)S(1)}, u32[]{:S(2)}, u32[]{:S(2)}) collective-permute-start(bf16[256,512]{1,0:T(8,128)(2,1)S(1)} %collective-permute-done.42.refs_2_), channel_id=1, source_target_pairs={{0,2},{1,3},{16,18},{17,19},{32,34},{33,35},{48,50},{49,51},{64,66... | collective-permute-start | bytes 786440 | tf_op jit(solution)/shard_map/ppermute | solution.py:24
  127.1 20.4 %collective-permute-start.47 = (bf16[256,512]{1,0:T(8,128)(2,1)S(1)}, bf16[256,512]{1,0:T(8,128)(2,1)S(1)}, u32[]{:S(2)}, u32[]{:S(2)}) collective-permute-start(bf16[256,512]{1,0:T(8,128)(2,1)S(1)} %collective-permute-done.45.refs_5_), channel_id=1, source_target_pairs={{0,6},{1,7},{16,22},{17,23},{32,38},{33,39},{48,54},{49,55},{64,70... | collective-permute-start | bytes 786440 | tf_op jit(solution)/shard_map/ppermute | solution.py:24
  129.7 12.7 %collective-permute-start.19 = (f16[256,256]{1,0:T(8,128)(2,1)S(1)}, f16[256,256]{1,0:T(8,128)(2,1)S(1)}, u32[]{:S(2)}, u32[]{:S(2)}) collective-permute-start(f16[256,256]{1,0:T(8,128)(2,1)S(1)} %get-tuple-element.23), channel_id=1, source_target_pairs={{0,10},{1,11},{16,26},{17,27},{32,42},{33,43},{48,58},{49,59},{64,... | collective-permute-start | bytes 393224 | tf_op jit(solution)/shard_map/ppermute | solution.py:24
  150.9 80.7 %collective-permute-start.49 = (bf16[2048,512]{1,0:T(8,128)(2,1)S(1)}, bf16[2048,512]{1,0:T(8,128)(2,1)}, u32[]{:S(2)}, u32[]{:S(2)}) collective-permute-start(bf16[2048,512]{1,0:T(8,128)(2,1)S(1)} %order_rows.3.refs_1_), channel_id=1, source_target_pairs={{0,1},{1,0},{16,17},{17,16},{32,33},{33,32},{48,49},{49,48},{64,65... | collective-permute-start | bytes 6291464 | tf_op jit(solution)/shard_map/ppermute | solution.py:24
  154.8 13.4 %collective-permute-start.26 = (bf16[256,256]{1,0:T(8,128)(2,1)S(1)}, bf16[256,256]{1,0:T(8,128)(2,1)S(1)}, u32[]{:S(2)}, u32[]{:S(2)}) collective-permute-start(bf16[256,256]{1,0:T(8,128)(2,1)S(1)} %fusion.26.refs_0_), channel_id=1, source_target_pairs={{0,2},{1,3},{16,18},{17,19},{32,34},{33,35},{48,50},{49,51},{64,66... | collective-permute-start | bytes 393224 | tf_op jit(solution)/shard_map/ppermute | solution.py:24
  157.6 12.0 %collective-permute-start.25 = (bf16[256,256]{1,0:T(8,128)(2,1)S(1)}, bf16[256,256]{1,0:T(8,128)(2,1)S(1)}, u32[]{:S(2)}, u32[]{:S(2)}) collective-permute-start(bf16[256,256]{1,0:T(8,128)(2,1)S(1)} %fusion.26.refs_0_), channel_id=1, source_target_pairs={{0,6},{1,7},{16,22},{17,23},{32,38},{33,39},{48,54},{49,55},{64,70... | collective-permute-start | bytes 393224 | tf_op jit(solution)/shard_map/ppermute | solution.py:24
  160.5 12.8 %collective-permute-start.29 = (bf16[256,256]{1,0:T(8,128)(2,1)S(1)}, bf16[256,256]{1,0:T(8,128)(2,1)S(1)}, u32[]{:S(2)}, u32[]{:S(2)}) collective-permute-start(bf16[256,256]{1,0:T(8,128)(2,1)S(1)} %collective-permute-done.28.refs_4_), channel_id=1, source_target_pairs={{0,6},{1,7},{16,22},{17,23},{32,38},{33,39},{48,54},{49,55},{64,70... | collective-permute-start | bytes 393224 | tf_op jit(solution)/shard_map/ppermute | solution.py:24
  168.2 11.0 %collective-permute-start.56 = (bf16[256,512]{1,0:T(8,128)(2,1)S(1)}, bf16[256,512]{1,0:T(8,128)(2,1)}, u32[]{:S(2)}, u32[]{:S(2)}) collective-permute-start(bf16[256,512]{1,0:T(8,128)(2,1)S(1)} %fusion.9.refs_0_), channel_id=1, source_target_pairs={{0,0},{1,1},{16,16},{17,17},{32,32},{33,33},{48,48},{49,49},{64,64... | collective-permute-start | bytes 786440 | tf_op jit(solution)/shard_map/ppermute | solution.py:24
  179.0 40.5 %collective-permute-start.48 = (bf16[2048,256]{1,0:T(8,128)(2,1)S(1)}, bf16[2048,256]{1,0:T(8,128)(2,1)}, u32[]{:S(2)}, u32[]{:S(2)}) collective-permute-start(bf16[2048,256]{1,0:T(8,128)(2,1)S(1)} %order_rows.2.refs_0_), channel_id=1, source_target_pairs={{0,1},{1,0},{16,17},{17,16},{32,33},{33,32},{48,49},{49,48},{64,65... | collective-permute-start | bytes 3145736 | tf_op jit(solution)/shard_map/ppermute | solution.py:24
  184.0 16.7 %collective-permute-start.66 = (bf16[256,512]{1,0:T(8,128)(2,1)S(1)}, bf16[256,512]{1,0:T(8,128)(2,1)S(1)}, u32[]{:S(2)}, u32[]{:S(2)}) collective-permute-start(bf16[256,512]{1,0:T(8,128)(2,1)S(1)} %collective-permute-done.57), channel_id=1, source_target_pairs={{1,64},{17,80},{33,96},{49,112},{64,1},{80,17},{96,33},{112,49},{9... | collective-permute-start | bytes 786440 | tf_op jit(solution)/shard_map/ppermute | solution.py:24
  184.7 19.7 %collective-permute-start.58 = (bf16[256,512]{1,0:T(8,128)(2,1)S(1)}, bf16[256,512]{1,0:T(8,128)(2,1)S(1)}, u32[]{:S(2)}, u32[]{:S(2)}) collective-permute-start(bf16[256,512]{1,0:T(8,128)(2,1)S(1)} %collective-permute-done.57), channel_id=1, source_target_pairs={{0,64},{1,0},{16,80},{17,16},{32,96},{33,32},{48,112},{49,48},{64,... | collective-permute-start | bytes 786440 | tf_op jit(solution)/shard_map/ppermute | solution.py:24
  207.4 15.4 %collective-permute-start.67 = (bf16[256,512]{1,0:T(8,128)(2,1)S(1)}, bf16[256,512]{1,0:T(8,128)(2,1)S(1)}, u32[]{:S(2)}, u32[]{:S(2)}) collective-permute-start(bf16[256,512]{1,0:T(8,128)(2,1)S(1)} %get-tuple-element.51.refs_16_), channel_id=1, source_target_pairs={{0,48},{1,49},{16,0},{17,1},{32,16},{33,17},{48,32},{49,33},{64,11... | collective-permute-start | bytes 786440 | tf_op jit(solution)/shard_map/ppermute | solution.py:24
  209.3 13.9 %collective-permute-start.60 = (bf16[256,512]{1,0:T(8,128)(2,1)S(1)}, bf16[256,512]{1,0:T(8,128)(2,1)S(1)}, u32[]{:S(2)}, u32[]{:S(2)}) collective-permute-start(bf16[256,512]{1,0:T(8,128)(2,1)S(1)} %get-tuple-element.52.refs_8_), channel_id=1, source_target_pairs={{0,16},{1,17},{16,32},{17,33},{32,48},{33,49},{48,0},{49,1},{64,80... | collective-permute-start | bytes 786440 | tf_op jit(solution)/shard_map/ppermute | solution.py:24
  (47 other events, 442.2 us)

commit v3 on v2

--- a/solution.py
+++ b/solution.py
@@ -9,7 +9,7 @@
 
 
 WIDTHS = (256, 512)
-ORDER = "SsRrYQ*yFqP+fMpmXUxONuZWnowzGVvgEe"
+ORDER = "SsRrYQ*yFqP+fMpmXUxONuZWnowzVvGgEe"
 SCALE = 64.0
 
 PLACES = [(x, h, l, z, c) for x in range(4) for h in range(2) for l in range(2) for z in range(4) for c in range(2)]
@@ -112,7 +112,7 @@
         ),
         compiler_params=pltpu.CompilerParams(vmem_limit_bytes=20 << 20),
         name="first",
-    )(meta, own, own, other, other, *pieces)
+    )(meta, *[pltpu.with_memory_space_constraint(own, pltpu.HBM)] * 2, other, other, *pieces)
 
 
 def order_rows_kernel(meta, *refs):
@@ -184,7 +184,7 @@
         ),
         compiler_params=pltpu.CompilerParams(vmem_limit_bytes=32 << 20),
         name="second",
-    )(meta, accumulated, gap_rows, gap_cols, *row_parts, *col_parts)
+    )(meta, pltpu.with_memory_space_constraint(accumulated, pltpu.HBM), gap_rows, gap_cols, *row_parts, *col_parts)
 
 
 def lookup(index, table):

time: 249 us -> 247 us (level)
  starting transfers between devices: 126 us -> 138 us
  waiting for transfers between devices: 79.5 us -> 68.8 us
  local copies, waits for them, and re-layouts: 9.69 us -> 4.12 us
  Pallas kernels: 24.5 us -> 27.1 us
    ppermute x70, starting transfers between devices: 126 us -> 138 us  [send(): return lax.ppermute(value, ('row', 'col'), pairs)]
    ppermute x70, waiting for transfers between devices: 79.5 us -> 68.8 us  [send(): return lax.ppermute(value, ('row', 'col'), pairs)]
    unnamed x18 -> x14, local copies, waits for them, and re-layouts: 5.6 us -> 0.03 us
where the time goes in v3:
time: 247 us; the launch traced here: 244 us
  starting transfers between devices  138 us (56%)
  waiting for transfers between devices  68.8 us (28%)
  Pallas kernels  27.1 us (11%)
  other arithmetic  5.87 us (2%)
  local copies, waits for them, and re-layouts  4.12 us (2%)
    ppermute x70, starting transfers between devices, send(): return lax.ppermute(value, ('row', 'col'), pairs)  138 us
    ppermute x70, waiting for transfers between devices, send(): return lax.ppermute(value, ('row', 'col'), pairs)  68.8 us
    pallas_call x2, Pallas kernels, first_product(): pl.pallas_call(first_kernel, out_shape=jax.ShapeDtypeStruct((8, rows, wid...  13.7 us
    pallas_call x1, Pallas kernels, second_product(): pl.pallas_call(functools.partial(second_kernel, widths), out_shape=jax.Sh...  12.1 us
  transfers between devices with their start and end apart: 70, of which 26 were waited for; matrix products, arithmetic and copies ran while one was open for 4% of the time, Pallas kernels for 3%

profile of v3, /device:TPU:0, one launch (start us, length us, event | category | flops | bytes accessed | tf_op | source)
XLA Modules:
  0.0 244.0 jit_solution(1347347445881325742)
XLA Ops:
  1.7 6.0 %collective-permute-done = bf16[128,768]{1,0:T(8,128)(2,1)S(1)} collective-permute-done((bf16[128,768]{1,0:T(8,128)(2,1)S(1)}, bf16[128,768]{1,0:T(8,128)(2,1)S(1)}, u32[]{:S(2)}, u32[]{:S(2)}) %collective-permute-start) | collective-permute-done | bytes 196640 | tf_op jit(solution)/shard_map/ppermute | solution.py:24
  12.4 8.4 %collective-permute-start.7 = (bf16[256,256]{1,0:T(8,128)(2,1)S(1)}, bf16[256,256]{1,0:T(8,128)(2,1)S(1)}, u32[]{:S(2)}, u32[]{:S(2)}) collective-permute-start(bf16[256,256]{1,0:T(8,128)(2,1)S(1)} %collective-permute-done.3.refs_4_), channel_id=1, source_target_pairs={{0,64},{1,65},{16,80},{17,81},{32,96},{33,97},{48,112},{49,113},{6... | collective-permute-start | bytes 393224 | tf_op jit(solution)/shard_map/ppermute | solution.py:24
  22.2 11.1 %collective-permute-start.5 = (bf16[256,256]{1,0:T(8,128)(2,1)S(1)}, bf16[256,256]{1,0:T(8,128)(2,1)S(1)}, u32[]{:S(2)}, u32[]{:S(2)}) collective-permute-start(bf16[256,256]{1,0:T(8,128)(2,1)S(1)} %collective-permute-done.3.refs_4_), channel_id=1, source_target_pairs={{0,16},{1,17},{16,32},{17,33},{32,48},{33,49},{48,0},{49,1},{64,80... | collective-permute-start | bytes 393224 | tf_op jit(solution)/shard_map/ppermute | solution.py:24
  33.3 5.2 %collective-permute-start.4 = (bf16[256,256]{1,0:T(8,128)(2,1)S(1)}, bf16[256,256]{1,0:T(8,128)(2,1)S(1)}, u32[]{:S(2)}, u32[]{:S(2)}) collective-permute-start(bf16[256,256]{1,0:T(8,128)(2,1)S(1)} %collective-permute-done.3.refs_4_), channel_id=1, source_target_pairs={{0,48},{1,49},{16,0},{17,1},{32,16},{33,17},{48,32},{49,33},{64,11... | collective-permute-start | bytes 393224 | tf_op jit(solution)/shard_map/ppermute | solution.py:24
  48.6 2.7 %collective-permute-done.9.refs_10_ = bf16[256,256]{1,0:T(8,128)(2,1)S(1)} collective-permute-done((bf16[256,256]{1,0:T(8,128)(2,1)S(1)}, bf16[256,256]{1,0:T(8,128)(2,1)S(1)}, u32[]{:S(2)}, u32[]{:S(2)}) %collective-permute-start.9) | collective-permute-done | bytes 131104 | tf_op jit(solution)/shard_map/ppermute | solution.py:24
  51.4 2.8 %collective-permute-done.6.refs_7_ = bf16[256,256]{1,0:T(8,128)(2,1)S(1)} collective-permute-done((bf16[256,256]{1,0:T(8,128)(2,1)S(1)}, bf16[256,256]{1,0:T(8,128)(2,1)S(1)}, u32[]{:S(2)}, u32[]{:S(2)}) %collective-permute-start.6) | collective-permute-done | bytes 131104 | tf_op jit(solution)/shard_map/ppermute | solution.py:24
  57.8 6.1 %first.2 = f32[8,256,256]{2,1,0:T(8,128)S(1)} custom-call(s32[32]{0:T(128)S(1)} %pad_add_fusion.meta, bf16[2048,1024]{1,0:T(8,128)(2,1)} %refs_1_.3, bf16[2048,1024]{1,0:T(8,128)(2,1)} %refs_1_.3, bf16[2048,1024]{1,0:T(8,128)(2,1)} %collective-permute-done.1.refs_2_.refs_3_, bf16[2048,1024]{1,0:T(8,128)(2,1)} %collective-permute-done.1.refs_2_.refs_3_, ...), custom_call_target="tpu_custom_call" | custom-call | flops 2147483648 | bytes 11534336 | tf_op jit(solution)/shard_map/first/pallas_call | solution.py:98
  66.2 3.2 %collective-permute-start.33 = (bf16[256,512]{1,0:T(8,128)(2,1)S(1)}, bf16[256,512]{1,0:T(8,128)(2,1)S(1)}, u32[]{:S(2)}, u32[]{:S(2)}) collective-permute-start(bf16[256,512]{1,0:T(8,128)(2,1)S(1)} %collective-permute-done.16.refs_9_), channel_id=1, source_target_pairs={{0,48},{1,49},{16,0},{17,1},{32,16},{33,17},{48,32},{49,33},{64,11... | collective-permute-start | bytes 786440 | tf_op jit(solution)/shard_map/ppermute | solution.py:24
  69.4 4.3 %collective-permute-done.32.refs_7_ = bf16[256,512]{1,0:T(8,128)(2,1)S(1)} collective-permute-done((bf16[256,512]{1,0:T(8,128)(2,1)S(1)}, bf16[256,512]{1,0:T(8,128)(2,1)S(1)}, u32[]{:S(2)}, u32[]{:S(2)}) %collective-permute-start.32) | collective-permute-done | bytes 262176 | tf_op jit(solution)/shard_map/ppermute | solution.py:24
  73.7 7.6 %first.3 = f32[8,256,512]{2,1,0:T(8,128)S(1)} custom-call(s32[32]{0:T(128)S(1)} %pad_add_fusion.meta, bf16[2048,1024]{1,0:T(8,128)(2,1)} %refs_1_.3, bf16[2048,1024]{1,0:T(8,128)(2,1)} %refs_1_.3, bf16[2048,1024]{1,0:T(8,128)(2,1)} %collective-permute-done.1.refs_2_.refs_3_, bf16[2048,1024]{1,0:T(8,128)(2,1)} %collective-permute-done.1.refs_2_.refs_3_, ...), custom_call_target="tpu_custom_call" | custom-call | flops 4294967296 | bytes 14680064 | tf_op jit(solution)/shard_map/first/pallas_call | solution.py:98
  85.9 3.3 %collective-permute-start.38 = (f16[256,512]{1,0:T(8,128)(2,1)S(1)}, f16[256,512]{1,0:T(8,128)(2,1)S(1)}, u32[]{:S(2)}, u32[]{:S(2)}) collective-permute-start(f16[256,512]{1,0:T(8,128)(2,1)S(1)} %get-tuple-element.38), channel_id=1, source_target_pairs={{0,4},{1,5},{16,20},{17,21},{32,36},{33,37},{48,52},{49,53},{64,68... | collective-permute-start | bytes 786440 | tf_op jit(solution)/shard_map/ppermute | solution.py:24
  90.5 4.5 %collective-permute-done.34 = f16[256,512]{1,0:T(8,128)(2,1)S(1)} collective-permute-done((f16[256,512]{1,0:T(8,128)(2,1)S(1)}, f16[256,512]{1,0:T(8,128)(2,1)S(1)}, u32[]{:S(2)}, u32[]{:S(2)}) %collective-permute-start.34) | collective-permute-done | bytes 262176 | tf_op jit(solution)/shard_map/ppermute | solution.py:24
  95.0 2.7 %collective-permute-start.36 = (f16[256,512]{1,0:T(8,128)(2,1)S(1)}, f16[256,512]{1,0:T(8,128)(2,1)S(1)}, u32[]{:S(2)}, u32[]{:S(2)}) collective-permute-start(f16[256,512]{1,0:T(8,128)(2,1)S(1)} %get-tuple-element.40), channel_id=1, source_target_pairs={{0,14},{1,15},{16,30},{17,31},{32,46},{33,47},{48,62},{49,63},{64,... | collective-permute-start | bytes 786440 | tf_op jit(solution)/shard_map/ppermute | solution.py:24
  100.1 3.7 %collective-permute-done.36 = f16[256,512]{1,0:T(8,128)(2,1)S(1)} collective-permute-done((f16[256,512]{1,0:T(8,128)(2,1)S(1)}, f16[256,512]{1,0:T(8,128)(2,1)S(1)}, u32[]{:S(2)}, u32[]{:S(2)}) %collective-permute-start.36) | collective-permute-done | bytes 262176 | tf_op jit(solution)/shard_map/ppermute | solution.py:24
  103.8 4.8 %collective-permute-done.35 = f16[256,512]{1,0:T(8,128)(2,1)S(1)} collective-permute-done((f16[256,512]{1,0:T(8,128)(2,1)S(1)}, f16[256,512]{1,0:T(8,128)(2,1)S(1)}, u32[]{:S(2)}, u32[]{:S(2)}) %collective-permute-start.35) | collective-permute-done | bytes 262176 | tf_op jit(solution)/shard_map/ppermute | solution.py:24
  111.1 6.1 %collective-permute-done.44.refs_4_ = bf16[256,512]{1,0:T(8,128)(2,1)S(1)} collective-permute-done((bf16[256,512]{1,0:T(8,128)(2,1)S(1)}, bf16[256,512]{1,0:T(8,128)(2,1)S(1)}, u32[]{:S(2)}, u32[]{:S(2)}) %collective-permute-start.44) | collective-permute-done | bytes 262176 | tf_op jit(solution)/shard_map/ppermute | solution.py:24
  117.2 4.1 %collective-permute-start.18 = (f16[256,256]{1,0:T(8,128)(2,1)S(1)}, f16[256,256]{1,0:T(8,128)(2,1)S(1)}, u32[]{:S(2)}, u32[]{:S(2)}) collective-permute-start(f16[256,256]{1,0:T(8,128)(2,1)S(1)} %get-tuple-element.22), channel_id=1, source_target_pairs={{0,12},{1,13},{16,28},{17,29},{32,44},{33,45},{48,60},{49,61},{64,... | collective-permute-start | bytes 393224 | tf_op jit(solution)/shard_map/ppermute | solution.py:24
  127.6 3.7 %collective-permute-start.19 = (f16[256,256]{1,0:T(8,128)(2,1)S(1)}, f16[256,256]{1,0:T(8,128)(2,1)S(1)}, u32[]{:S(2)}, u32[]{:S(2)}) collective-permute-start(f16[256,256]{1,0:T(8,128)(2,1)S(1)} %get-tuple-element.23), channel_id=1, source_target_pairs={{0,10},{1,11},{16,26},{17,27},{32,42},{33,43},{48,58},{49,59},{64,... | collective-permute-start | bytes 393224 | tf_op jit(solution)/shard_map/ppermute | solution.py:24
  131.3 7.4 %collective-permute-done.19 = f16[256,256]{1,0:T(8,128)(2,1)S(1)} collective-permute-done((f16[256,256]{1,0:T(8,128)(2,1)S(1)}, f16[256,256]{1,0:T(8,128)(2,1)S(1)}, u32[]{:S(2)}, u32[]{:S(2)}) %collective-permute-start.19) | collective-permute-done | bytes 131104 | tf_op jit(solution)/shard_map/ppermute | solution.py:24
  145.1 2.7 %collective-permute-start.24 = (f16[256,256]{1,0:T(8,128)(2,1)S(1)}, f16[256,256]{1,0:T(8,128)(2,1)S(1)}, u32[]{:S(2)}, u32[]{:S(2)}) collective-permute-start(f16[256,256]{1,0:T(8,128)(2,1)S(1)} %get-tuple-element.28), channel_id=1, source_target_pairs={{0,6},{1,7},{16,22},{17,23},{32,38},{33,39},{48,54},{49,55},{64,70... | collective-permute-start | bytes 393224 | tf_op jit(solution)/shard_map/ppermute | solution.py:24
  152.8 4.2 %collective-permute-start.26 = (bf16[256,256]{1,0:T(8,128)(2,1)S(1)}, bf16[256,256]{1,0:T(8,128)(2,1)S(1)}, u32[]{:S(2)}, u32[]{:S(2)}) collective-permute-start(bf16[256,256]{1,0:T(8,128)(2,1)S(1)} %fusion.26.refs_0_), channel_id=1, source_target_pairs={{0,2},{1,3},{16,18},{17,19},{32,34},{33,35},{48,50},{49,51},{64,66... | collective-permute-start | bytes 393224 | tf_op jit(solution)/shard_map/ppermute | solution.py:24
  160.1 5.0 %collective-permute-start.29 = (bf16[256,256]{1,0:T(8,128)(2,1)S(1)}, bf16[256,256]{1,0:T(8,128)(2,1)S(1)}, u32[]{:S(2)}, u32[]{:S(2)}) collective-permute-start(bf16[256,256]{1,0:T(8,128)(2,1)S(1)} %collective-permute-done.28.refs_4_), channel_id=1, source_target_pairs={{0,6},{1,7},{16,22},{17,23},{32,38},{33,39},{48,54},{49,55},{64,70... | collective-permute-start | bytes 393224 | tf_op jit(solution)/shard_map/ppermute | solution.py:24
  167.0 2.6 %collective-permute-start.27 = (bf16[256,256]{1,0:T(8,128)(2,1)S(1)}, bf16[256,256]{1,0:T(8,128)(2,1)S(1)}, u32[]{:S(2)}, u32[]{:S(2)}) collective-permute-start(bf16[256,256]{1,0:T(8,128)(2,1)S(1)} %collective-permute-done.26.refs_2_), channel_id=1, source_target_pairs={{0,2},{1,3},{16,18},{17,19},{32,34},{33,35},{48,50},{49,51},{64,66... | collective-permute-start | bytes 393224 | tf_op jit(solution)/shard_map/ppermute | solution.py:24
  174.1 5.1 %collective-permute-start.52 = (bf16[256,256]{1,0:T(8,128)(2,1)S(1)}, bf16[256,256]{1,0:T(8,128)(2,1)}, u32[]{:S(2)}, u32[]{:S(2)}) collective-permute-start(bf16[256,256]{1,0:T(8,128)(2,1)S(1)} %collective-permute-done.51), channel_id=1, source_target_pairs={{0,64},{1,0},{16,80},{17,16},{32,96},{33,32},{48,112},{49,48},{64,... | collective-permute-start | bytes 393224 | tf_op jit(solution)/shard_map/ppermute | solution.py:24
  184.2 10.0 %collective-permute-start.58 = (bf16[256,512]{1,0:T(8,128)(2,1)S(1)}, bf16[256,512]{1,0:T(8,128)(2,1)S(1)}, u32[]{:S(2)}, u32[]{:S(2)}) collective-permute-start(bf16[256,512]{1,0:T(8,128)(2,1)S(1)} %collective-permute-done.57), channel_id=1, source_target_pairs={{0,64},{1,0},{16,80},{17,16},{32,96},{33,32},{48,112},{49,48},{64,... | collective-permute-start | bytes 786440 | tf_op jit(solution)/shard_map/ppermute | solution.py:24
  194.2 3.7 %collective-permute-start.63 = (bf16[256,256]{1,0:T(8,128)(2,1)S(1)}, bf16[256,256]{1,0:T(8,128)(2,1)S(1)}, u32[]{:S(2)}, u32[]{:S(2)}) collective-permute-start(bf16[256,256]{1,0:T(8,128)(2,1)S(1)} %get-tuple-element.53.refs_12_), channel_id=1, source_target_pairs={{0,48},{1,49},{16,0},{17,1},{32,16},{33,17},{48,32},{49,33},{64,11... | collective-permute-start | bytes 393224 | tf_op jit(solution)/shard_map/ppermute | solution.py:24
  197.9 3.1 %collective-permute-done.63.refs_13_ = bf16[256,256]{1,0:T(8,128)(2,1)S(1)} collective-permute-done((bf16[256,256]{1,0:T(8,128)(2,1)S(1)}, bf16[256,256]{1,0:T(8,128)(2,1)S(1)}, u32[]{:S(2)}, u32[]{:S(2)}) %collective-permute-start.63) | collective-permute-done | bytes 131104 | tf_op jit(solution)/shard_map/ppermute | solution.py:24
  201.1 3.6 %collective-permute-start.53 = (bf16[256,256]{1,0:T(8,128)(2,1)S(1)}, bf16[256,256]{1,0:T(8,128)(2,1)S(1)}, u32[]{:S(2)}, u32[]{:S(2)}) collective-permute-start(bf16[256,256]{1,0:T(8,128)(2,1)S(1)} %get-tuple-element.54.refs_4_), channel_id=1, source_target_pairs={{0,48},{1,49},{16,0},{17,1},{32,16},{33,17},{48,32},{49,33},{64,11... | collective-permute-start | bytes 393224 | tf_op jit(solution)/shard_map/ppermute | solution.py:24
  213.3 6.5 %collective-permute-done.55.refs_7_ = bf16[256,256]{1,0:T(8,128)(2,1)S(1)} collective-permute-done((bf16[256,256]{1,0:T(8,128)(2,1)S(1)}, bf16[256,256]{1,0:T(8,128)(2,1)S(1)}, u32[]{:S(2)}, u32[]{:S(2)}) %collective-permute-start.55) | collective-permute-done | bytes 131104 | tf_op jit(solution)/shard_map/ppermute | solution.py:24
  219.8 3.2 %collective-permute-start.59 = (bf16[256,512]{1,0:T(8,128)(2,1)S(1)}, bf16[256,512]{1,0:T(8,128)(2,1)S(1)}, u32[]{:S(2)}, u32[]{:S(2)}) collective-permute-start(bf16[256,512]{1,0:T(8,128)(2,1)S(1)} %get-tuple-element.52.refs_8_), channel_id=1, source_target_pairs={{0,48},{1,49},{16,0},{17,1},{32,16},{33,17},{48,32},{49,33},{64,11... | collective-permute-start | bytes 786440 | tf_op jit(solution)/shard_map/ppermute | solution.py:24
  225.1 4.0 %collective-permute-done.68.refs_18_ = bf16[256,512]{1,0:T(8,128)(2,1)S(1)} collective-permute-done((bf16[256,512]{1,0:T(8,128)(2,1)S(1)}, bf16[256,512]{1,0:T(8,128)(2,1)S(1)}, u32[]{:S(2)}, u32[]{:S(2)}) %collective-permute-start.68) | collective-permute-done | bytes 262176 | tf_op jit(solution)/shard_map/ppermute | solution.py:24
  231.9 12.1 %second.1 = f32[2048,1024]{1,0:T(8,128)} custom-call(s32[32]{0:T(128)S(1)} %pad_add_fusion.meta, f32[2048,1024]{1,0:T(8,128)} %acc_ref.1, f32[2048,128]{1,0:T(8,128)S(1)} %copy-done, f32[1,1024]{1,0:T(1,128)S(1)} %bitcast.58, bf16[2048,256]{1,0:T(8,128)(2,1)S(1)} %order_rows.2.refs_0_, bf16[2048,512]{1,0:T(8,128)(2,1)S(1)} %order_rows.3.refs_1_, ...), custom_call_target="tpu_custom_call" | custom-call | flops 6442450944 | bytes 26214400 | tf_op jit(solution)/shard_map/second/pallas_call | solution.py:164
  (151 shorter events, 79.9 us)
Async XLA Ops:
  0.0 57.8 %collective-permute-start.1 = (bf16[2048,1024]{1,0:T(8,128)(2,1)}, bf16[2048,1024]{1,0:T(8,128)(2,1)}, u32[]{:S(2)}, u32[]{:S(2)}) collective-permute-start(bf16[2048,1024]{1,0:T(8,128)(2,1)} %refs_1_.3), channel_id=1, source_target_pairs={{0,1},{1,0},{16,17},{17,16},{32,33},{33,32},{48,49},{49,48},{64,65... | collective-permute-start | bytes 12582920 | tf_op jit(solution)/shard_map/ppermute | solution.py:24
  9.5 11.3 %collective-permute-start.11 = (bf16[256,512]{1,0:T(8,128)(2,1)S(1)}, bf16[256,512]{1,0:T(8,128)(2,1)S(1)}, u32[]{:S(2)}, u32[]{:S(2)}) collective-permute-start(bf16[256,512]{1,0:T(8,128)(2,1)S(1)} %pad_maximum_fusion), channel_id=1, source_target_pairs={{0,0},{1,1},{16,16},{17,17},{32,32},{33,33},{48,48},{49,49},{64,64... | collective-permute-start | bytes 786440 | tf_op jit(solution)/shard_map/ppermute | solution.py:24
  12.4 26.1 %collective-permute-start.7 = (bf16[256,256]{1,0:T(8,128)(2,1)S(1)}, bf16[256,256]{1,0:T(8,128)(2,1)S(1)}, u32[]{:S(2)}, u32[]{:S(2)}) collective-permute-start(bf16[256,256]{1,0:T(8,128)(2,1)S(1)} %collective-permute-done.3.refs_4_), channel_id=1, source_target_pairs={{0,64},{1,65},{16,80},{17,81},{32,96},{33,97},{48,112},{49,113},{6... | collective-permute-start | bytes 393224 | tf_op jit(solution)/shard_map/ppermute | solution.py:24
  20.8 20.7 %collective-permute-start.12 = (bf16[256,512]{1,0:T(8,128)(2,1)S(1)}, bf16[256,512]{1,0:T(8,128)(2,1)S(1)}, u32[]{:S(2)}, u32[]{:S(2)}) collective-permute-start(bf16[256,512]{1,0:T(8,128)(2,1)S(1)} %collective-permute-done.11), channel_id=1, source_target_pairs={{0,0},{1,1},{16,18},{17,19},{32,36},{33,37},{48,54},{49,55},{64,8}... | collective-permute-start | bytes 786440 | tf_op jit(solution)/shard_map/ppermute | solution.py:24
  22.2 21.5 %collective-permute-start.5 = (bf16[256,256]{1,0:T(8,128)(2,1)S(1)}, bf16[256,256]{1,0:T(8,128)(2,1)S(1)}, u32[]{:S(2)}, u32[]{:S(2)}) collective-permute-start(bf16[256,256]{1,0:T(8,128)(2,1)S(1)} %collective-permute-done.3.refs_4_), channel_id=1, source_target_pairs={{0,16},{1,17},{16,32},{17,33},{32,48},{33,49},{48,0},{49,1},{64,80... | collective-permute-start | bytes 393224 | tf_op jit(solution)/shard_map/ppermute | solution.py:24
  33.3 10.6 %collective-permute-start.4 = (bf16[256,256]{1,0:T(8,128)(2,1)S(1)}, bf16[256,256]{1,0:T(8,128)(2,1)S(1)}, u32[]{:S(2)}, u32[]{:S(2)}) collective-permute-start(bf16[256,256]{1,0:T(8,128)(2,1)S(1)} %collective-permute-done.3.refs_4_), channel_id=1, source_target_pairs={{0,48},{1,49},{16,0},{17,1},{32,16},{33,17},{48,32},{49,33},{64,11... | collective-permute-start | bytes 393224 | tf_op jit(solution)/shard_map/ppermute | solution.py:24
  41.5 13.1 %collective-permute-start.15 = (bf16[256,512]{1,0:T(8,128)(2,1)S(1)}, bf16[256,512]{1,0:T(8,128)(2,1)S(1)}, u32[]{:S(2)}, u32[]{:S(2)}) collective-permute-start(bf16[256,512]{1,0:T(8,128)(2,1)S(1)} %collective-permute-done.12.refs_4_), channel_id=1, source_target_pairs={{0,64},{1,65},{16,80},{17,81},{32,96},{33,97},{48,112},{49,113},{6... | collective-permute-start | bytes 786440 | tf_op jit(solution)/shard_map/ppermute | solution.py:24
  43.9 10.3 %collective-permute-start.6 = (bf16[256,256]{1,0:T(8,128)(2,1)S(1)}, bf16[256,256]{1,0:T(8,128)(2,1)S(1)}, u32[]{:S(2)}, u32[]{:S(2)}) collective-permute-start(bf16[256,256]{1,0:T(8,128)(2,1)S(1)} %collective-permute-done.5.refs_6_), channel_id=1, source_target_pairs={{0,16},{1,17},{16,32},{17,33},{32,48},{33,49},{48,0},{49,1},{64,80... | collective-permute-start | bytes 393224 | tf_op jit(solution)/shard_map/ppermute | solution.py:24
  44.9 11.3 %collective-permute-start.10 = (bf16[256,256]{1,0:T(8,128)(2,1)S(1)}, bf16[256,256]{1,0:T(8,128)(2,1)S(1)}, u32[]{:S(2)}, u32[]{:S(2)}) collective-permute-start(bf16[256,256]{1,0:T(8,128)(2,1)S(1)} %collective-permute-done.8.refs_9_), channel_id=1, source_target_pairs={{0,48},{1,49},{16,0},{17,1},{32,16},{33,17},{48,32},{49,33},{64,11... | collective-permute-start | bytes 393224 | tf_op jit(solution)/shard_map/ppermute | solution.py:24
  51.4 12.8 %collective-permute-start.14 = (bf16[256,512]{1,0:T(8,128)(2,1)S(1)}, bf16[256,512]{1,0:T(8,128)(2,1)S(1)}, u32[]{:S(2)}, u32[]{:S(2)}) collective-permute-start(bf16[256,512]{1,0:T(8,128)(2,1)S(1)} %collective-permute-done.12.refs_4_), channel_id=1, source_target_pairs={{0,16},{1,17},{16,32},{17,33},{32,48},{33,49},{48,0},{49,1},{64,80... | collective-permute-start | bytes 786440 | tf_op jit(solution)/shard_map/ppermute | solution.py:24
  81.9 13.1 %collective-permute-start.34 = (f16[256,512]{1,0:T(8,128)(2,1)S(1)}, f16[256,512]{1,0:T(8,128)(2,1)S(1)}, u32[]{:S(2)}, u32[]{:S(2)}) collective-permute-start(f16[256,512]{1,0:T(8,128)(2,1)S(1)} %get-tuple-element.35), channel_id=1, source_target_pairs={{0,12},{1,13},{16,28},{17,29},{32,44},{33,45},{48,60},{49,61},{64,... | collective-permute-start | bytes 786440 | tf_op jit(solution)/shard_map/ppermute | solution.py:24
  83.9 13.8 %collective-permute-start.40 = (f16[256,512]{1,0:T(8,128)(2,1)S(1)}, f16[256,512]{1,0:T(8,128)(2,1)S(1)}, u32[]{:S(2)}, u32[]{:S(2)}) collective-permute-start(f16[256,512]{1,0:T(8,128)(2,1)S(1)} %get-tuple-element.36), channel_id=1, source_target_pairs={{0,6},{1,7},{16,22},{17,23},{32,38},{33,39},{48,54},{49,55},{64,70... | collective-permute-start | bytes 786440 | tf_op jit(solution)/shard_map/ppermute | solution.py:24
  83.9 16.1 %collective-permute-start.39 = (f16[256,512]{1,0:T(8,128)(2,1)S(1)}, f16[256,512]{1,0:T(8,128)(2,1)S(1)}, u32[]{:S(2)}, u32[]{:S(2)}) collective-permute-start(f16[256,512]{1,0:T(8,128)(2,1)S(1)} %get-tuple-element.37), channel_id=1, source_target_pairs={{0,2},{1,3},{16,18},{17,19},{32,34},{33,35},{48,50},{49,51},{64,66... | collective-permute-start | bytes 786440 | tf_op jit(solution)/shard_map/ppermute | solution.py:24
  85.9 14.1 %collective-permute-start.38 = (f16[256,512]{1,0:T(8,128)(2,1)S(1)}, f16[256,512]{1,0:T(8,128)(2,1)S(1)}, u32[]{:S(2)}, u32[]{:S(2)}) collective-permute-start(f16[256,512]{1,0:T(8,128)(2,1)S(1)} %get-tuple-element.38), channel_id=1, source_target_pairs={{0,4},{1,5},{16,20},{17,21},{32,36},{33,37},{48,52},{49,53},{64,68... | collective-permute-start | bytes 786440 | tf_op jit(solution)/shard_map/ppermute | solution.py:24
  89.3 10.9 %collective-permute-start.37 = (f16[256,512]{1,0:T(8,128)(2,1)S(1)}, f16[256,512]{1,0:T(8,128)(2,1)S(1)}, u32[]{:S(2)}, u32[]{:S(2)}) collective-permute-start(f16[256,512]{1,0:T(8,128)(2,1)S(1)} %get-tuple-element.39), channel_id=1, source_target_pairs={{0,8},{1,9},{16,24},{17,25},{32,40},{33,41},{48,56},{49,57},{64,72... | collective-permute-start | bytes 786440 | tf_op jit(solution)/shard_map/ppermute | solution.py:24
  97.7 10.9 %collective-permute-start.35 = (f16[256,512]{1,0:T(8,128)(2,1)S(1)}, f16[256,512]{1,0:T(8,128)(2,1)S(1)}, u32[]{:S(2)}, u32[]{:S(2)}) collective-permute-start(f16[256,512]{1,0:T(8,128)(2,1)S(1)} %get-tuple-element.41), channel_id=1, source_target_pairs={{0,10},{1,11},{16,26},{17,27},{32,42},{33,43},{48,58},{49,59},{64,... | collective-permute-start | bytes 786440 | tf_op jit(solution)/shard_map/ppermute | solution.py:24
  110.1 13.3 %collective-permute-start.42 = (bf16[256,512]{1,0:T(8,128)(2,1)S(1)}, bf16[256,512]{1,0:T(8,128)(2,1)S(1)}, u32[]{:S(2)}, u32[]{:S(2)}) collective-permute-start(bf16[256,512]{1,0:T(8,128)(2,1)S(1)} %fusion.9.refs_0_), channel_id=1, source_target_pairs={{0,2},{1,3},{16,18},{17,19},{32,34},{33,35},{48,50},{49,51},{64,66... | collective-permute-start | bytes 786440 | tf_op jit(solution)/shard_map/ppermute | solution.py:24
  117.2 10.4 %collective-permute-start.18 = (f16[256,256]{1,0:T(8,128)(2,1)S(1)}, f16[256,256]{1,0:T(8,128)(2,1)S(1)}, u32[]{:S(2)}, u32[]{:S(2)}) collective-permute-start(f16[256,256]{1,0:T(8,128)(2,1)S(1)} %get-tuple-element.22), channel_id=1, source_target_pairs={{0,12},{1,13},{16,28},{17,29},{32,44},{33,45},{48,60},{49,61},{64,... | collective-permute-start | bytes 393224 | tf_op jit(solution)/shard_map/ppermute | solution.py:24
  121.3 18.5 %collective-permute-start.41 = (bf16[256,512]{1,0:T(8,128)(2,1)S(1)}, bf16[256,512]{1,0:T(8,128)(2,1)S(1)}, u32[]{:S(2)}, u32[]{:S(2)}) collective-permute-start(bf16[256,512]{1,0:T(8,128)(2,1)S(1)} %fusion.9.refs_0_), channel_id=1, source_target_pairs={{0,6},{1,7},{16,22},{17,23},{32,38},{33,39},{48,54},{49,55},{64,70... | collective-permute-start | bytes 786440 | tf_op jit(solution)/shard_map/ppermute | solution.py:24
  122.1 20.2 %collective-permute-start.46 = (bf16[256,512]{1,0:T(8,128)(2,1)S(1)}, bf16[256,512]{1,0:T(8,128)(2,1)S(1)}, u32[]{:S(2)}, u32[]{:S(2)}) collective-permute-start(bf16[256,512]{1,0:T(8,128)(2,1)S(1)} %collective-permute-done.44.refs_4_), channel_id=1, source_target_pairs={{0,2},{1,3},{16,18},{17,19},{32,34},{33,35},{48,50},{49,51},{64,66... | collective-permute-start | bytes 786440 | tf_op jit(solution)/shard_map/ppermute | solution.py:24
  123.4 21.2 %collective-permute-start.43 = (bf16[256,512]{1,0:T(8,128)(2,1)S(1)}, bf16[256,512]{1,0:T(8,128)(2,1)S(1)}, u32[]{:S(2)}, u32[]{:S(2)}) collective-permute-start(bf16[256,512]{1,0:T(8,128)(2,1)S(1)} %collective-permute-done.42.refs_2_), channel_id=1, source_target_pairs={{0,2},{1,3},{16,18},{17,19},{32,34},{33,35},{48,50},{49,51},{64,66... | collective-permute-start | bytes 786440 | tf_op jit(solution)/shard_map/ppermute | solution.py:24
  125.0 20.1 %collective-permute-start.47 = (bf16[256,512]{1,0:T(8,128)(2,1)S(1)}, bf16[256,512]{1,0:T(8,128)(2,1)S(1)}, u32[]{:S(2)}, u32[]{:S(2)}) collective-permute-start(bf16[256,512]{1,0:T(8,128)(2,1)S(1)} %collective-permute-done.45.refs_5_), channel_id=1, source_target_pairs={{0,6},{1,7},{16,22},{17,23},{32,38},{33,39},{48,54},{49,55},{64,70... | collective-permute-start | bytes 786440 | tf_op jit(solution)/shard_map/ppermute | solution.py:24
  127.6 11.0 %collective-permute-start.19 = (f16[256,256]{1,0:T(8,128)(2,1)S(1)}, f16[256,256]{1,0:T(8,128)(2,1)S(1)}, u32[]{:S(2)}, u32[]{:S(2)}) collective-permute-start(f16[256,256]{1,0:T(8,128)(2,1)S(1)} %get-tuple-element.23), channel_id=1, source_target_pairs={{0,10},{1,11},{16,26},{17,27},{32,42},{33,43},{48,58},{49,59},{64,... | collective-permute-start | bytes 393224 | tf_op jit(solution)/shard_map/ppermute | solution.py:24
  148.5 83.4 %collective-permute-start.49 = (bf16[2048,512]{1,0:T(8,128)(2,1)S(1)}, bf16[2048,512]{1,0:T(8,128)(2,1)}, u32[]{:S(2)}, u32[]{:S(2)}) collective-permute-start(bf16[2048,512]{1,0:T(8,128)(2,1)S(1)} %order_rows.3.refs_1_), channel_id=1, source_target_pairs={{0,1},{1,0},{16,17},{17,16},{32,33},{33,32},{48,49},{49,48},{64,65... | collective-permute-start | bytes 6291464 | tf_op jit(solution)/shard_map/ppermute | solution.py:24
  152.8 12.4 %collective-permute-start.26 = (bf16[256,256]{1,0:T(8,128)(2,1)S(1)}, bf16[256,256]{1,0:T(8,128)(2,1)S(1)}, u32[]{:S(2)}, u32[]{:S(2)}) collective-permute-start(bf16[256,256]{1,0:T(8,128)(2,1)S(1)} %fusion.26.refs_0_), channel_id=1, source_target_pairs={{0,2},{1,3},{16,18},{17,19},{32,34},{33,35},{48,50},{49,51},{64,66... | collective-permute-start | bytes 393224 | tf_op jit(solution)/shard_map/ppermute | solution.py:24
  165.2 14.9 %collective-permute-start.56 = (bf16[256,512]{1,0:T(8,128)(2,1)S(1)}, bf16[256,512]{1,0:T(8,128)(2,1)}, u32[]{:S(2)}, u32[]{:S(2)}) collective-permute-start(bf16[256,512]{1,0:T(8,128)(2,1)S(1)} %fusion.9.refs_0_), channel_id=1, source_target_pairs={{0,0},{1,1},{16,16},{17,17},{32,32},{33,33},{48,48},{49,49},{64,64... | collective-permute-start | bytes 786440 | tf_op jit(solution)/shard_map/ppermute | solution.py:24
  179.9 39.9 %collective-permute-start.48 = (bf16[2048,256]{1,0:T(8,128)(2,1)S(1)}, bf16[2048,256]{1,0:T(8,128)(2,1)}, u32[]{:S(2)}, u32[]{:S(2)}) collective-permute-start(bf16[2048,256]{1,0:T(8,128)(2,1)S(1)} %order_rows.2.refs_0_), channel_id=1, source_target_pairs={{0,1},{1,0},{16,17},{17,16},{32,33},{33,32},{48,49},{49,48},{64,65... | collective-permute-start | bytes 3145736 | tf_op jit(solution)/shard_map/ppermute | solution.py:24
  183.4 10.8 %collective-permute-start.64 = (bf16[256,256]{1,0:T(8,128)(2,1)S(1)}, bf16[256,256]{1,0:T(8,128)(2,1)S(1)}, u32[]{:S(2)}, u32[]{:S(2)}) collective-permute-start(bf16[256,256]{1,0:T(8,128)(2,1)S(1)} %get-tuple-element.53.refs_12_), channel_id=1, source_target_pairs={{0,16},{1,17},{16,32},{17,33},{32,48},{33,49},{48,0},{49,1},{64,80... | collective-permute-start | bytes 393224 | tf_op jit(solution)/shard_map/ppermute | solution.py:24
  183.5 17.6 %collective-permute-start.66 = (bf16[256,512]{1,0:T(8,128)(2,1)S(1)}, bf16[256,512]{1,0:T(8,128)(2,1)S(1)}, u32[]{:S(2)}, u32[]{:S(2)}) collective-permute-start(bf16[256,512]{1,0:T(8,128)(2,1)S(1)} %collective-permute-done.57), channel_id=1, source_target_pairs={{1,64},{17,80},{33,96},{49,112},{64,1},{80,17},{96,33},{112,49},{9... | collective-permute-start | bytes 786440 | tf_op jit(solution)/shard_map/ppermute | solution.py:24
  184.2 20.5 %collective-permute-start.58 = (bf16[256,512]{1,0:T(8,128)(2,1)S(1)}, bf16[256,512]{1,0:T(8,128)(2,1)S(1)}, u32[]{:S(2)}, u32[]{:S(2)}) collective-permute-start(bf16[256,512]{1,0:T(8,128)(2,1)S(1)} %collective-permute-done.57), channel_id=1, source_target_pairs={{0,64},{1,0},{16,80},{17,16},{32,96},{33,32},{48,112},{49,48},{64,... | collective-permute-start | bytes 786440 | tf_op jit(solution)/shard_map/ppermute | solution.py:24
  207.7 15.4 %collective-permute-start.67 = (bf16[256,512]{1,0:T(8,128)(2,1)S(1)}, bf16[256,512]{1,0:T(8,128)(2,1)S(1)}, u32[]{:S(2)}, u32[]{:S(2)}) collective-permute-start(bf16[256,512]{1,0:T(8,128)(2,1)S(1)} %get-tuple-element.51.refs_16_), channel_id=1, source_target_pairs={{0,48},{1,49},{16,0},{17,1},{32,16},{33,17},{48,32},{49,33},{64,11... | collective-permute-start | bytes 786440 | tf_op jit(solution)/shard_map/ppermute | solution.py:24
  209.7 13.9 %collective-permute-start.60 = (bf16[256,512]{1,0:T(8,128)(2,1)S(1)}, bf16[256,512]{1,0:T(8,128)(2,1)S(1)}, u32[]{:S(2)}, u32[]{:S(2)}) collective-permute-start(bf16[256,512]{1,0:T(8,128)(2,1)S(1)} %get-tuple-element.52.refs_8_), channel_id=1, source_target_pairs={{0,16},{1,17},{16,32},{17,33},{32,48},{33,49},{48,0},{49,1},{64,80... | collective-permute-start | bytes 786440 | tf_op jit(solution)/shard_map/ppermute | solution.py:24
  (45 other events, 445.6 us)

commit v4 on v3

--- a/solution.py
+++ b/solution.py
@@ -293,9 +293,8 @@
     env.meta = jnp.concatenate([destinations, sources, mine, (z + ring - x) & 3])
 
     half = cholesky.shape[1] // 2
-    low, high = cholesky[:, :half], cholesky[:, half:]
-    keep = jnp.where(c == 0, low, high)
-    got = send(jnp.where(c == 0, high, low), other_core)
+    keep = lax.dynamic_slice_in_dim(cholesky, c * half, half, 1)
+    got = send(lax.dynamic_slice_in_dim(cholesky, (1 - c) * half, half, 1), other_core)
     b_piece = jnp.concatenate([jnp.where(c == 0, keep, got), jnp.where(c == 0, got, keep)], axis=0)
     env.own = amplitudes
 

time: 247 us -> 247 us (level)
  no operation moved by 1% of the time
where the time goes in v4:
time: 247 us; the launch traced here: 244 us
  starting transfers between devices  138 us (56%)
  waiting for transfers between devices  68.9 us (28%)
  Pallas kernels  27.1 us (11%)
  local copies, waits for them, and re-layouts  5.07 us (2%)
  other arithmetic  4.76 us (2%)
    ppermute x70, starting transfers between devices, send(): return lax.ppermute(value, ('row', 'col'), pairs)  138 us
    ppermute x70, waiting for transfers between devices, send(): return lax.ppermute(value, ('row', 'col'), pairs)  68.9 us
    pallas_call x2, Pallas kernels, first_product(): pl.pallas_call(first_kernel, out_shape=jax.ShapeDtypeStruct((8, rows, wid...  13.7 us
    pallas_call x1, Pallas kernels, second_product(): pl.pallas_call(functools.partial(second_kernel, widths), out_shape=jax.Sh...  12.1 us
  transfers between devices with their start and end apart: 70, of which 26 were waited for; matrix products, arithmetic and copies ran while one was open for 4% of the time, Pallas kernels for 3%

profile of v4, /device:TPU:0, one launch (start us, length us, event | category | flops | bytes accessed | tf_op | source)
XLA Modules:
  0.0 243.9 jit_solution(11511140817938851541)
XLA Ops:
  1.6 6.1 %collective-permute-done = bf16[128,768]{1,0:T(8,128)(2,1)S(1)} collective-permute-done((bf16[128,768]{1,0:T(8,128)(2,1)S(1)}, bf16[128,768]{1,0:T(8,128)(2,1)S(1)}, u32[]{:S(2)}, u32[]{:S(2)}) %collective-permute-start) | collective-permute-done | bytes 196640 | tf_op jit(solution)/shard_map/ppermute | solution.py:24
  12.3 8.4 %collective-permute-start.7 = (bf16[256,256]{1,0:T(8,128)(2,1)S(1)}, bf16[256,256]{1,0:T(8,128)(2,1)S(1)}, u32[]{:S(2)}, u32[]{:S(2)}) collective-permute-start(bf16[256,256]{1,0:T(8,128)(2,1)S(1)} %collective-permute-done.3.refs_4_), channel_id=1, source_target_pairs={{0,64},{1,65},{16,80},{17,81},{32,96},{33,97},{48,112},{49,113},{6... | collective-permute-start | bytes 393224 | tf_op jit(solution)/shard_map/ppermute | solution.py:24
  22.2 11.1 %collective-permute-start.5 = (bf16[256,256]{1,0:T(8,128)(2,1)S(1)}, bf16[256,256]{1,0:T(8,128)(2,1)S(1)}, u32[]{:S(2)}, u32[]{:S(2)}) collective-permute-start(bf16[256,256]{1,0:T(8,128)(2,1)S(1)} %collective-permute-done.3.refs_4_), channel_id=1, source_target_pairs={{0,16},{1,17},{16,32},{17,33},{32,48},{33,49},{48,0},{49,1},{64,80... | collective-permute-start | bytes 393224 | tf_op jit(solution)/shard_map/ppermute | solution.py:24
  33.2 5.2 %collective-permute-start.4 = (bf16[256,256]{1,0:T(8,128)(2,1)S(1)}, bf16[256,256]{1,0:T(8,128)(2,1)S(1)}, u32[]{:S(2)}, u32[]{:S(2)}) collective-permute-start(bf16[256,256]{1,0:T(8,128)(2,1)S(1)} %collective-permute-done.3.refs_4_), channel_id=1, source_target_pairs={{0,48},{1,49},{16,0},{17,1},{32,16},{33,17},{48,32},{49,33},{64,11... | collective-permute-start | bytes 393224 | tf_op jit(solution)/shard_map/ppermute | solution.py:24
  48.6 2.7 %collective-permute-done.9.refs_10_ = bf16[256,256]{1,0:T(8,128)(2,1)S(1)} collective-permute-done((bf16[256,256]{1,0:T(8,128)(2,1)S(1)}, bf16[256,256]{1,0:T(8,128)(2,1)S(1)}, u32[]{:S(2)}, u32[]{:S(2)}) %collective-permute-start.9) | collective-permute-done | bytes 131104 | tf_op jit(solution)/shard_map/ppermute | solution.py:24
  51.3 2.8 %collective-permute-done.6.refs_7_ = bf16[256,256]{1,0:T(8,128)(2,1)S(1)} collective-permute-done((bf16[256,256]{1,0:T(8,128)(2,1)S(1)}, bf16[256,256]{1,0:T(8,128)(2,1)S(1)}, u32[]{:S(2)}, u32[]{:S(2)}) %collective-permute-start.6) | collective-permute-done | bytes 131104 | tf_op jit(solution)/shard_map/ppermute | solution.py:24
  57.8 6.1 %first.2 = f32[8,256,256]{2,1,0:T(8,128)S(1)} custom-call(s32[32]{0:T(128)S(1)} %pad_add_fusion.meta, bf16[2048,1024]{1,0:T(8,128)(2,1)} %refs_1_.3, bf16[2048,1024]{1,0:T(8,128)(2,1)} %refs_1_.3, bf16[2048,1024]{1,0:T(8,128)(2,1)} %collective-permute-done.1.refs_2_.refs_3_, bf16[2048,1024]{1,0:T(8,128)(2,1)} %collective-permute-done.1.refs_2_.refs_3_, ...), custom_call_target="tpu_custom_call" | custom-call | flops 2147483648 | bytes 11534336 | tf_op jit(solution)/shard_map/first/pallas_call | solution.py:98
  66.1 3.2 %collective-permute-start.33 = (bf16[256,512]{1,0:T(8,128)(2,1)S(1)}, bf16[256,512]{1,0:T(8,128)(2,1)S(1)}, u32[]{:S(2)}, u32[]{:S(2)}) collective-permute-start(bf16[256,512]{1,0:T(8,128)(2,1)S(1)} %collective-permute-done.16.refs_9_), channel_id=1, source_target_pairs={{0,48},{1,49},{16,0},{17,1},{32,16},{33,17},{48,32},{49,33},{64,11... | collective-permute-start | bytes 786440 | tf_op jit(solution)/shard_map/ppermute | solution.py:24
  69.3 4.3 %collective-permute-done.32.refs_7_ = bf16[256,512]{1,0:T(8,128)(2,1)S(1)} collective-permute-done((bf16[256,512]{1,0:T(8,128)(2,1)S(1)}, bf16[256,512]{1,0:T(8,128)(2,1)S(1)}, u32[]{:S(2)}, u32[]{:S(2)}) %collective-permute-start.32) | collective-permute-done | bytes 262176 | tf_op jit(solution)/shard_map/ppermute | solution.py:24
  73.7 7.6 %first.3 = f32[8,256,512]{2,1,0:T(8,128)S(1)} custom-call(s32[32]{0:T(128)S(1)} %pad_add_fusion.meta, bf16[2048,1024]{1,0:T(8,128)(2,1)} %refs_1_.3, bf16[2048,1024]{1,0:T(8,128)(2,1)} %refs_1_.3, bf16[2048,1024]{1,0:T(8,128)(2,1)} %collective-permute-done.1.refs_2_.refs_3_, bf16[2048,1024]{1,0:T(8,128)(2,1)} %collective-permute-done.1.refs_2_.refs_3_, ...), custom_call_target="tpu_custom_call" | custom-call | flops 4294967296 | bytes 14680064 | tf_op jit(solution)/shard_map/first/pallas_call | solution.py:98
  85.9 3.3 %collective-permute-start.38 = (f16[256,512]{1,0:T(8,128)(2,1)S(1)}, f16[256,512]{1,0:T(8,128)(2,1)S(1)}, u32[]{:S(2)}, u32[]{:S(2)}) collective-permute-start(f16[256,512]{1,0:T(8,128)(2,1)S(1)} %get-tuple-element.38), channel_id=1, source_target_pairs={{0,4},{1,5},{16,20},{17,21},{32,36},{33,37},{48,52},{49,53},{64,68... | collective-permute-start | bytes 786440 | tf_op jit(solution)/shard_map/ppermute | solution.py:24
  90.5 4.5 %collective-permute-done.34 = f16[256,512]{1,0:T(8,128)(2,1)S(1)} collective-permute-done((f16[256,512]{1,0:T(8,128)(2,1)S(1)}, f16[256,512]{1,0:T(8,128)(2,1)S(1)}, u32[]{:S(2)}, u32[]{:S(2)}) %collective-permute-start.34) | collective-permute-done | bytes 262176 | tf_op jit(solution)/shard_map/ppermute | solution.py:24
  95.0 2.7 %collective-permute-start.36 = (f16[256,512]{1,0:T(8,128)(2,1)S(1)}, f16[256,512]{1,0:T(8,128)(2,1)S(1)}, u32[]{:S(2)}, u32[]{:S(2)}) collective-permute-start(f16[256,512]{1,0:T(8,128)(2,1)S(1)} %get-tuple-element.40), channel_id=1, source_target_pairs={{0,14},{1,15},{16,30},{17,31},{32,46},{33,47},{48,62},{49,63},{64,... | collective-permute-start | bytes 786440 | tf_op jit(solution)/shard_map/ppermute | solution.py:24
  100.1 3.7 %collective-permute-done.36 = f16[256,512]{1,0:T(8,128)(2,1)S(1)} collective-permute-done((f16[256,512]{1,0:T(8,128)(2,1)S(1)}, f16[256,512]{1,0:T(8,128)(2,1)S(1)}, u32[]{:S(2)}, u32[]{:S(2)}) %collective-permute-start.36) | collective-permute-done | bytes 262176 | tf_op jit(solution)/shard_map/ppermute | solution.py:24
  103.7 4.8 %collective-permute-done.35 = f16[256,512]{1,0:T(8,128)(2,1)S(1)} collective-permute-done((f16[256,512]{1,0:T(8,128)(2,1)S(1)}, f16[256,512]{1,0:T(8,128)(2,1)S(1)}, u32[]{:S(2)}, u32[]{:S(2)}) %collective-permute-start.35) | collective-permute-done | bytes 262176 | tf_op jit(solution)/shard_map/ppermute | solution.py:24
  111.0 6.1 %collective-permute-done.44.refs_4_ = bf16[256,512]{1,0:T(8,128)(2,1)S(1)} collective-permute-done((bf16[256,512]{1,0:T(8,128)(2,1)S(1)}, bf16[256,512]{1,0:T(8,128)(2,1)S(1)}, u32[]{:S(2)}, u32[]{:S(2)}) %collective-permute-start.44) | collective-permute-done | bytes 262176 | tf_op jit(solution)/shard_map/ppermute | solution.py:24
  117.2 4.1 %collective-permute-start.18 = (f16[256,256]{1,0:T(8,128)(2,1)S(1)}, f16[256,256]{1,0:T(8,128)(2,1)S(1)}, u32[]{:S(2)}, u32[]{:S(2)}) collective-permute-start(f16[256,256]{1,0:T(8,128)(2,1)S(1)} %get-tuple-element.22), channel_id=1, source_target_pairs={{0,12},{1,13},{16,28},{17,29},{32,44},{33,45},{48,60},{49,61},{64,... | collective-permute-start | bytes 393224 | tf_op jit(solution)/shard_map/ppermute | solution.py:24
  127.5 3.7 %collective-permute-start.19 = (f16[256,256]{1,0:T(8,128)(2,1)S(1)}, f16[256,256]{1,0:T(8,128)(2,1)S(1)}, u32[]{:S(2)}, u32[]{:S(2)}) collective-permute-start(f16[256,256]{1,0:T(8,128)(2,1)S(1)} %get-tuple-element.23), channel_id=1, source_target_pairs={{0,10},{1,11},{16,26},{17,27},{32,42},{33,43},{48,58},{49,59},{64,... | collective-permute-start | bytes 393224 | tf_op jit(solution)/shard_map/ppermute | solution.py:24
  131.2 7.4 %collective-permute-done.19 = f16[256,256]{1,0:T(8,128)(2,1)S(1)} collective-permute-done((f16[256,256]{1,0:T(8,128)(2,1)S(1)}, f16[256,256]{1,0:T(8,128)(2,1)S(1)}, u32[]{:S(2)}, u32[]{:S(2)}) %collective-permute-start.19) | collective-permute-done | bytes 131104 | tf_op jit(solution)/shard_map/ppermute | solution.py:24
  145.1 2.7 %collective-permute-start.24 = (f16[256,256]{1,0:T(8,128)(2,1)S(1)}, f16[256,256]{1,0:T(8,128)(2,1)S(1)}, u32[]{:S(2)}, u32[]{:S(2)}) collective-permute-start(f16[256,256]{1,0:T(8,128)(2,1)S(1)} %get-tuple-element.28), channel_id=1, source_target_pairs={{0,6},{1,7},{16,22},{17,23},{32,38},{33,39},{48,54},{49,55},{64,70... | collective-permute-start | bytes 393224 | tf_op jit(solution)/shard_map/ppermute | solution.py:24
  152.7 4.1 %collective-permute-start.26 = (bf16[256,256]{1,0:T(8,128)(2,1)S(1)}, bf16[256,256]{1,0:T(8,128)(2,1)S(1)}, u32[]{:S(2)}, u32[]{:S(2)}) collective-permute-start(bf16[256,256]{1,0:T(8,128)(2,1)S(1)} %fusion.26.refs_0_), channel_id=1, source_target_pairs={{0,2},{1,3},{16,18},{17,19},{32,34},{33,35},{48,50},{49,51},{64,66... | collective-permute-start | bytes 393224 | tf_op jit(solution)/shard_map/ppermute | solution.py:24
  160.1 5.0 %collective-permute-start.29 = (bf16[256,256]{1,0:T(8,128)(2,1)S(1)}, bf16[256,256]{1,0:T(8,128)(2,1)S(1)}, u32[]{:S(2)}, u32[]{:S(2)}) collective-permute-start(bf16[256,256]{1,0:T(8,128)(2,1)S(1)} %collective-permute-done.28.refs_4_), channel_id=1, source_target_pairs={{0,6},{1,7},{16,22},{17,23},{32,38},{33,39},{48,54},{49,55},{64,70... | collective-permute-start | bytes 393224 | tf_op jit(solution)/shard_map/ppermute | solution.py:24
  166.9 2.6 %collective-permute-start.27 = (bf16[256,256]{1,0:T(8,128)(2,1)S(1)}, bf16[256,256]{1,0:T(8,128)(2,1)S(1)}, u32[]{:S(2)}, u32[]{:S(2)}) collective-permute-start(bf16[256,256]{1,0:T(8,128)(2,1)S(1)} %collective-permute-done.26.refs_2_), channel_id=1, source_target_pairs={{0,2},{1,3},{16,18},{17,19},{32,34},{33,35},{48,50},{49,51},{64,66... | collective-permute-start | bytes 393224 | tf_op jit(solution)/shard_map/ppermute | solution.py:24
  174.1 5.1 %collective-permute-start.52 = (bf16[256,256]{1,0:T(8,128)(2,1)S(1)}, bf16[256,256]{1,0:T(8,128)(2,1)}, u32[]{:S(2)}, u32[]{:S(2)}) collective-permute-start(bf16[256,256]{1,0:T(8,128)(2,1)S(1)} %collective-permute-done.51), channel_id=1, source_target_pairs={{0,64},{1,0},{16,80},{17,16},{32,96},{33,32},{48,112},{49,48},{64,... | collective-permute-start | bytes 393224 | tf_op jit(solution)/shard_map/ppermute | solution.py:24
  184.1 10.0 %collective-permute-start.58 = (bf16[256,512]{1,0:T(8,128)(2,1)S(1)}, bf16[256,512]{1,0:T(8,128)(2,1)S(1)}, u32[]{:S(2)}, u32[]{:S(2)}) collective-permute-start(bf16[256,512]{1,0:T(8,128)(2,1)S(1)} %collective-permute-done.57), channel_id=1, source_target_pairs={{0,64},{1,0},{16,80},{17,16},{32,96},{33,32},{48,112},{49,48},{64,... | collective-permute-start | bytes 786440 | tf_op jit(solution)/shard_map/ppermute | solution.py:24
  194.1 3.7 %collective-permute-start.63 = (bf16[256,256]{1,0:T(8,128)(2,1)S(1)}, bf16[256,256]{1,0:T(8,128)(2,1)S(1)}, u32[]{:S(2)}, u32[]{:S(2)}) collective-permute-start(bf16[256,256]{1,0:T(8,128)(2,1)S(1)} %get-tuple-element.53.refs_12_), channel_id=1, source_target_pairs={{0,48},{1,49},{16,0},{17,1},{32,16},{33,17},{48,32},{49,33},{64,11... | collective-permute-start | bytes 393224 | tf_op jit(solution)/shard_map/ppermute | solution.py:24
  197.8 3.1 %collective-permute-done.63.refs_13_ = bf16[256,256]{1,0:T(8,128)(2,1)S(1)} collective-permute-done((bf16[256,256]{1,0:T(8,128)(2,1)S(1)}, bf16[256,256]{1,0:T(8,128)(2,1)S(1)}, u32[]{:S(2)}, u32[]{:S(2)}) %collective-permute-start.63) | collective-permute-done | bytes 131104 | tf_op jit(solution)/shard_map/ppermute | solution.py:24
  201.1 3.5 %collective-permute-start.53 = (bf16[256,256]{1,0:T(8,128)(2,1)S(1)}, bf16[256,256]{1,0:T(8,128)(2,1)S(1)}, u32[]{:S(2)}, u32[]{:S(2)}) collective-permute-start(bf16[256,256]{1,0:T(8,128)(2,1)S(1)} %get-tuple-element.54.refs_4_), channel_id=1, source_target_pairs={{0,48},{1,49},{16,0},{17,1},{32,16},{33,17},{48,32},{49,33},{64,11... | collective-permute-start | bytes 393224 | tf_op jit(solution)/shard_map/ppermute | solution.py:24
  213.2 6.5 %collective-permute-done.55.refs_7_ = bf16[256,256]{1,0:T(8,128)(2,1)S(1)} collective-permute-done((bf16[256,256]{1,0:T(8,128)(2,1)S(1)}, bf16[256,256]{1,0:T(8,128)(2,1)S(1)}, u32[]{:S(2)}, u32[]{:S(2)}) %collective-permute-start.55) | collective-permute-done | bytes 131104 | tf_op jit(solution)/shard_map/ppermute | solution.py:24
  219.7 3.2 %collective-permute-start.59 = (bf16[256,512]{1,0:T(8,128)(2,1)S(1)}, bf16[256,512]{1,0:T(8,128)(2,1)S(1)}, u32[]{:S(2)}, u32[]{:S(2)}) collective-permute-start(bf16[256,512]{1,0:T(8,128)(2,1)S(1)} %get-tuple-element.52.refs_8_), channel_id=1, source_target_pairs={{0,48},{1,49},{16,0},{17,1},{32,16},{33,17},{48,32},{49,33},{64,11... | collective-permute-start | bytes 786440 | tf_op jit(solution)/shard_map/ppermute | solution.py:24
  225.0 4.0 %collective-permute-done.68.refs_18_ = bf16[256,512]{1,0:T(8,128)(2,1)S(1)} collective-permute-done((bf16[256,512]{1,0:T(8,128)(2,1)S(1)}, bf16[256,512]{1,0:T(8,128)(2,1)S(1)}, u32[]{:S(2)}, u32[]{:S(2)}) %collective-permute-start.68) | collective-permute-done | bytes 262176 | tf_op jit(solution)/shard_map/ppermute | solution.py:24
  231.8 12.1 %second.1 = f32[2048,1024]{1,0:T(8,128)} custom-call(s32[32]{0:T(128)S(1)} %pad_add_fusion.meta, f32[2048,1024]{1,0:T(8,128)} %acc_ref.1, f32[2048,128]{1,0:T(8,128)S(1)} %copy-done, f32[1,1024]{1,0:T(1,128)S(1)} %bitcast.58, bf16[2048,256]{1,0:T(8,128)(2,1)S(1)} %order_rows.2.refs_0_, bf16[2048,512]{1,0:T(8,128)(2,1)S(1)} %order_rows.3.refs_1_, ...), custom_call_target="tpu_custom_call" | custom-call | flops 6442450944 | bytes 26214400 | tf_op jit(solution)/shard_map/second/pallas_call | solution.py:164
  (151 shorter events, 79.8 us)
Async XLA Ops:
  0.0 57.8 %collective-permute-start.1 = (bf16[2048,1024]{1,0:T(8,128)(2,1)}, bf16[2048,1024]{1,0:T(8,128)(2,1)}, u32[]{:S(2)}, u32[]{:S(2)}) collective-permute-start(bf16[2048,1024]{1,0:T(8,128)(2,1)} %refs_1_.3), channel_id=1, source_target_pairs={{0,1},{1,0},{16,17},{17,16},{32,33},{33,32},{48,49},{49,48},{64,65... | collective-permute-start | bytes 12582920 | tf_op jit(solution)/shard_map/ppermute | solution.py:24
  9.5 11.3 %collective-permute-start.11 = (bf16[256,512]{1,0:T(8,128)(2,1)S(1)}, bf16[256,512]{1,0:T(8,128)(2,1)S(1)}, u32[]{:S(2)}, u32[]{:S(2)}) collective-permute-start(bf16[256,512]{1,0:T(8,128)(2,1)S(1)} %pad_maximum_fusion), channel_id=1, source_target_pairs={{0,0},{1,1},{16,16},{17,17},{32,32},{33,33},{48,48},{49,49},{64,64... | collective-permute-start | bytes 786440 | tf_op jit(solution)/shard_map/ppermute | solution.py:24
  12.3 26.1 %collective-permute-start.7 = (bf16[256,256]{1,0:T(8,128)(2,1)S(1)}, bf16[256,256]{1,0:T(8,128)(2,1)S(1)}, u32[]{:S(2)}, u32[]{:S(2)}) collective-permute-start(bf16[256,256]{1,0:T(8,128)(2,1)S(1)} %collective-permute-done.3.refs_4_), channel_id=1, source_target_pairs={{0,64},{1,65},{16,80},{17,81},{32,96},{33,97},{48,112},{49,113},{6... | collective-permute-start | bytes 393224 | tf_op jit(solution)/shard_map/ppermute | solution.py:24
  20.8 20.7 %collective-permute-start.12 = (bf16[256,512]{1,0:T(8,128)(2,1)S(1)}, bf16[256,512]{1,0:T(8,128)(2,1)S(1)}, u32[]{:S(2)}, u32[]{:S(2)}) collective-permute-start(bf16[256,512]{1,0:T(8,128)(2,1)S(1)} %collective-permute-done.11), channel_id=1, source_target_pairs={{0,0},{1,1},{16,18},{17,19},{32,36},{33,37},{48,54},{49,55},{64,8}... | collective-permute-start | bytes 786440 | tf_op jit(solution)/shard_map/ppermute | solution.py:24
  22.2 21.5 %collective-permute-start.5 = (bf16[256,256]{1,0:T(8,128)(2,1)S(1)}, bf16[256,256]{1,0:T(8,128)(2,1)S(1)}, u32[]{:S(2)}, u32[]{:S(2)}) collective-permute-start(bf16[256,256]{1,0:T(8,128)(2,1)S(1)} %collective-permute-done.3.refs_4_), channel_id=1, source_target_pairs={{0,16},{1,17},{16,32},{17,33},{32,48},{33,49},{48,0},{49,1},{64,80... | collective-permute-start | bytes 393224 | tf_op jit(solution)/shard_map/ppermute | solution.py:24
  33.2 10.6 %collective-permute-start.4 = (bf16[256,256]{1,0:T(8,128)(2,1)S(1)}, bf16[256,256]{1,0:T(8,128)(2,1)S(1)}, u32[]{:S(2)}, u32[]{:S(2)}) collective-permute-start(bf16[256,256]{1,0:T(8,128)(2,1)S(1)} %collective-permute-done.3.refs_4_), channel_id=1, source_target_pairs={{0,48},{1,49},{16,0},{17,1},{32,16},{33,17},{48,32},{49,33},{64,11... | collective-permute-start | bytes 393224 | tf_op jit(solution)/shard_map/ppermute | solution.py:24
  41.5 13.1 %collective-permute-start.15 = (bf16[256,512]{1,0:T(8,128)(2,1)S(1)}, bf16[256,512]{1,0:T(8,128)(2,1)S(1)}, u32[]{:S(2)}, u32[]{:S(2)}) collective-permute-start(bf16[256,512]{1,0:T(8,128)(2,1)S(1)} %collective-permute-done.12.refs_4_), channel_id=1, source_target_pairs={{0,64},{1,65},{16,80},{17,81},{32,96},{33,97},{48,112},{49,113},{6... | collective-permute-start | bytes 786440 | tf_op jit(solution)/shard_map/ppermute | solution.py:24
  43.8 10.3 %collective-permute-start.6 = (bf16[256,256]{1,0:T(8,128)(2,1)S(1)}, bf16[256,256]{1,0:T(8,128)(2,1)S(1)}, u32[]{:S(2)}, u32[]{:S(2)}) collective-permute-start(bf16[256,256]{1,0:T(8,128)(2,1)S(1)} %collective-permute-done.5.refs_6_), channel_id=1, source_target_pairs={{0,16},{1,17},{16,32},{17,33},{32,48},{33,49},{48,0},{49,1},{64,80... | collective-permute-start | bytes 393224 | tf_op jit(solution)/shard_map/ppermute | solution.py:24
  44.9 11.3 %collective-permute-start.10 = (bf16[256,256]{1,0:T(8,128)(2,1)S(1)}, bf16[256,256]{1,0:T(8,128)(2,1)S(1)}, u32[]{:S(2)}, u32[]{:S(2)}) collective-permute-start(bf16[256,256]{1,0:T(8,128)(2,1)S(1)} %collective-permute-done.8.refs_9_), channel_id=1, source_target_pairs={{0,48},{1,49},{16,0},{17,1},{32,16},{33,17},{48,32},{49,33},{64,11... | collective-permute-start | bytes 393224 | tf_op jit(solution)/shard_map/ppermute | solution.py:24
  51.3 12.8 %collective-permute-start.14 = (bf16[256,512]{1,0:T(8,128)(2,1)S(1)}, bf16[256,512]{1,0:T(8,128)(2,1)S(1)}, u32[]{:S(2)}, u32[]{:S(2)}) collective-permute-start(bf16[256,512]{1,0:T(8,128)(2,1)S(1)} %collective-permute-done.12.refs_4_), channel_id=1, source_target_pairs={{0,16},{1,17},{16,32},{17,33},{32,48},{33,49},{48,0},{49,1},{64,80... | collective-permute-start | bytes 786440 | tf_op jit(solution)/shard_map/ppermute | solution.py:24
  81.9 13.1 %collective-permute-start.34 = (f16[256,512]{1,0:T(8,128)(2,1)S(1)}, f16[256,512]{1,0:T(8,128)(2,1)S(1)}, u32[]{:S(2)}, u32[]{:S(2)}) collective-permute-start(f16[256,512]{1,0:T(8,128)(2,1)S(1)} %get-tuple-element.35), channel_id=1, source_target_pairs={{0,12},{1,13},{16,28},{17,29},{32,44},{33,45},{48,60},{49,61},{64,... | collective-permute-start | bytes 786440 | tf_op jit(solution)/shard_map/ppermute | solution.py:24
  83.9 13.8 %collective-permute-start.40 = (f16[256,512]{1,0:T(8,128)(2,1)S(1)}, f16[256,512]{1,0:T(8,128)(2,1)S(1)}, u32[]{:S(2)}, u32[]{:S(2)}) collective-permute-start(f16[256,512]{1,0:T(8,128)(2,1)S(1)} %get-tuple-element.36), channel_id=1, source_target_pairs={{0,6},{1,7},{16,22},{17,23},{32,38},{33,39},{48,54},{49,55},{64,70... | collective-permute-start | bytes 786440 | tf_op jit(solution)/shard_map/ppermute | solution.py:24
  83.9 16.1 %collective-permute-start.39 = (f16[256,512]{1,0:T(8,128)(2,1)S(1)}, f16[256,512]{1,0:T(8,128)(2,1)S(1)}, u32[]{:S(2)}, u32[]{:S(2)}) collective-permute-start(f16[256,512]{1,0:T(8,128)(2,1)S(1)} %get-tuple-element.37), channel_id=1, source_target_pairs={{0,2},{1,3},{16,18},{17,19},{32,34},{33,35},{48,50},{49,51},{64,66... | collective-permute-start | bytes 786440 | tf_op jit(solution)/shard_map/ppermute | solution.py:24
  85.9 14.1 %collective-permute-start.38 = (f16[256,512]{1,0:T(8,128)(2,1)S(1)}, f16[256,512]{1,0:T(8,128)(2,1)S(1)}, u32[]{:S(2)}, u32[]{:S(2)}) collective-permute-start(f16[256,512]{1,0:T(8,128)(2,1)S(1)} %get-tuple-element.38), channel_id=1, source_target_pairs={{0,4},{1,5},{16,20},{17,21},{32,36},{33,37},{48,52},{49,53},{64,68... | collective-permute-start | bytes 786440 | tf_op jit(solution)/shard_map/ppermute | solution.py:24
  89.2 10.9 %collective-permute-start.37 = (f16[256,512]{1,0:T(8,128)(2,1)S(1)}, f16[256,512]{1,0:T(8,128)(2,1)S(1)}, u32[]{:S(2)}, u32[]{:S(2)}) collective-permute-start(f16[256,512]{1,0:T(8,128)(2,1)S(1)} %get-tuple-element.39), channel_id=1, source_target_pairs={{0,8},{1,9},{16,24},{17,25},{32,40},{33,41},{48,56},{49,57},{64,72... | collective-permute-start | bytes 786440 | tf_op jit(solution)/shard_map/ppermute | solution.py:24
  97.7 10.9 %collective-permute-start.35 = (f16[256,512]{1,0:T(8,128)(2,1)S(1)}, f16[256,512]{1,0:T(8,128)(2,1)S(1)}, u32[]{:S(2)}, u32[]{:S(2)}) collective-permute-start(f16[256,512]{1,0:T(8,128)(2,1)S(1)} %get-tuple-element.41), channel_id=1, source_target_pairs={{0,10},{1,11},{16,26},{17,27},{32,42},{33,43},{48,58},{49,59},{64,... | collective-permute-start | bytes 786440 | tf_op jit(solution)/shard_map/ppermute | solution.py:24
  110.1 13.3 %collective-permute-start.42 = (bf16[256,512]{1,0:T(8,128)(2,1)S(1)}, bf16[256,512]{1,0:T(8,128)(2,1)S(1)}, u32[]{:S(2)}, u32[]{:S(2)}) collective-permute-start(bf16[256,512]{1,0:T(8,128)(2,1)S(1)} %fusion.9.refs_0_), channel_id=1, source_target_pairs={{0,2},{1,3},{16,18},{17,19},{32,34},{33,35},{48,50},{49,51},{64,66... | collective-permute-start | bytes 786440 | tf_op jit(solution)/shard_map/ppermute | solution.py:24
  117.2 10.4 %collective-permute-start.18 = (f16[256,256]{1,0:T(8,128)(2,1)S(1)}, f16[256,256]{1,0:T(8,128)(2,1)S(1)}, u32[]{:S(2)}, u32[]{:S(2)}) collective-permute-start(f16[256,256]{1,0:T(8,128)(2,1)S(1)} %get-tuple-element.22), channel_id=1, source_target_pairs={{0,12},{1,13},{16,28},{17,29},{32,44},{33,45},{48,60},{49,61},{64,... | collective-permute-start | bytes 393224 | tf_op jit(solution)/shard_map/ppermute | solution.py:24
  121.3 18.5 %collective-permute-start.41 = (bf16[256,512]{1,0:T(8,128)(2,1)S(1)}, bf16[256,512]{1,0:T(8,128)(2,1)S(1)}, u32[]{:S(2)}, u32[]{:S(2)}) collective-permute-start(bf16[256,512]{1,0:T(8,128)(2,1)S(1)} %fusion.9.refs_0_), channel_id=1, source_target_pairs={{0,6},{1,7},{16,22},{17,23},{32,38},{33,39},{48,54},{49,55},{64,70... | collective-permute-start | bytes 786440 | tf_op jit(solution)/shard_map/ppermute | solution.py:24
  122.1 20.2 %collective-permute-start.46 = (bf16[256,512]{1,0:T(8,128)(2,1)S(1)}, bf16[256,512]{1,0:T(8,128)(2,1)S(1)}, u32[]{:S(2)}, u32[]{:S(2)}) collective-permute-start(bf16[256,512]{1,0:T(8,128)(2,1)S(1)} %collective-permute-done.44.refs_4_), channel_id=1, source_target_pairs={{0,2},{1,3},{16,18},{17,19},{32,34},{33,35},{48,50},{49,51},{64,66... | collective-permute-start | bytes 786440 | tf_op jit(solution)/shard_map/ppermute | solution.py:24
  123.3 21.2 %collective-permute-start.43 = (bf16[256,512]{1,0:T(8,128)(2,1)S(1)}, bf16[256,512]{1,0:T(8,128)(2,1)S(1)}, u32[]{:S(2)}, u32[]{:S(2)}) collective-permute-start(bf16[256,512]{1,0:T(8,128)(2,1)S(1)} %collective-permute-done.42.refs_2_), channel_id=1, source_target_pairs={{0,2},{1,3},{16,18},{17,19},{32,34},{33,35},{48,50},{49,51},{64,66... | collective-permute-start | bytes 786440 | tf_op jit(solution)/shard_map/ppermute | solution.py:24
  125.0 20.1 %collective-permute-start.47 = (bf16[256,512]{1,0:T(8,128)(2,1)S(1)}, bf16[256,512]{1,0:T(8,128)(2,1)S(1)}, u32[]{:S(2)}, u32[]{:S(2)}) collective-permute-start(bf16[256,512]{1,0:T(8,128)(2,1)S(1)} %collective-permute-done.45.refs_5_), channel_id=1, source_target_pairs={{0,6},{1,7},{16,22},{17,23},{32,38},{33,39},{48,54},{49,55},{64,70... | collective-permute-start | bytes 786440 | tf_op jit(solution)/shard_map/ppermute | solution.py:24
  127.5 11.0 %collective-permute-start.19 = (f16[256,256]{1,0:T(8,128)(2,1)S(1)}, f16[256,256]{1,0:T(8,128)(2,1)S(1)}, u32[]{:S(2)}, u32[]{:S(2)}) collective-permute-start(f16[256,256]{1,0:T(8,128)(2,1)S(1)} %get-tuple-element.23), channel_id=1, source_target_pairs={{0,10},{1,11},{16,26},{17,27},{32,42},{33,43},{48,58},{49,59},{64,... | collective-permute-start | bytes 393224 | tf_op jit(solution)/shard_map/ppermute | solution.py:24
  148.5 83.3 %collective-permute-start.49 = (bf16[2048,512]{1,0:T(8,128)(2,1)S(1)}, bf16[2048,512]{1,0:T(8,128)(2,1)}, u32[]{:S(2)}, u32[]{:S(2)}) collective-permute-start(bf16[2048,512]{1,0:T(8,128)(2,1)S(1)} %order_rows.3.refs_1_), channel_id=1, source_target_pairs={{0,1},{1,0},{16,17},{17,16},{32,33},{33,32},{48,49},{49,48},{64,65... | collective-permute-start | bytes 6291464 | tf_op jit(solution)/shard_map/ppermute | solution.py:24
  152.7 12.4 %collective-permute-start.26 = (bf16[256,256]{1,0:T(8,128)(2,1)S(1)}, bf16[256,256]{1,0:T(8,128)(2,1)S(1)}, u32[]{:S(2)}, u32[]{:S(2)}) collective-permute-start(bf16[256,256]{1,0:T(8,128)(2,1)S(1)} %fusion.26.refs_0_), channel_id=1, source_target_pairs={{0,2},{1,3},{16,18},{17,19},{32,34},{33,35},{48,50},{49,51},{64,66... | collective-permute-start | bytes 393224 | tf_op jit(solution)/shard_map/ppermute | solution.py:24
  165.1 14.9 %collective-permute-start.56 = (bf16[256,512]{1,0:T(8,128)(2,1)S(1)}, bf16[256,512]{1,0:T(8,128)(2,1)}, u32[]{:S(2)}, u32[]{:S(2)}) collective-permute-start(bf16[256,512]{1,0:T(8,128)(2,1)S(1)} %fusion.9.refs_0_), channel_id=1, source_target_pairs={{0,0},{1,1},{16,16},{17,17},{32,32},{33,33},{48,48},{49,49},{64,64... | collective-permute-start | bytes 786440 | tf_op jit(solution)/shard_map/ppermute | solution.py:24
  179.8 39.9 %collective-permute-start.48 = (bf16[2048,256]{1,0:T(8,128)(2,1)S(1)}, bf16[2048,256]{1,0:T(8,128)(2,1)}, u32[]{:S(2)}, u32[]{:S(2)}) collective-permute-start(bf16[2048,256]{1,0:T(8,128)(2,1)S(1)} %order_rows.2.refs_0_), channel_id=1, source_target_pairs={{0,1},{1,0},{16,17},{17,16},{32,33},{33,32},{48,49},{49,48},{64,65... | collective-permute-start | bytes 3145736 | tf_op jit(solution)/shard_map/ppermute | solution.py:24
  183.3 10.8 %collective-permute-start.64 = (bf16[256,256]{1,0:T(8,128)(2,1)S(1)}, bf16[256,256]{1,0:T(8,128)(2,1)S(1)}, u32[]{:S(2)}, u32[]{:S(2)}) collective-permute-start(bf16[256,256]{1,0:T(8,128)(2,1)S(1)} %get-tuple-element.53.refs_12_), channel_id=1, source_target_pairs={{0,16},{1,17},{16,32},{17,33},{32,48},{33,49},{48,0},{49,1},{64,80... | collective-permute-start | bytes 393224 | tf_op jit(solution)/shard_map/ppermute | solution.py:24
  183.4 17.7 %collective-permute-start.66 = (bf16[256,512]{1,0:T(8,128)(2,1)S(1)}, bf16[256,512]{1,0:T(8,128)(2,1)S(1)}, u32[]{:S(2)}, u32[]{:S(2)}) collective-permute-start(bf16[256,512]{1,0:T(8,128)(2,1)S(1)} %collective-permute-done.57), channel_id=1, source_target_pairs={{1,64},{17,80},{33,96},{49,112},{64,1},{80,17},{96,33},{112,49},{9... | collective-permute-start | bytes 786440 | tf_op jit(solution)/shard_map/ppermute | solution.py:24
  184.1 20.5 %collective-permute-start.58 = (bf16[256,512]{1,0:T(8,128)(2,1)S(1)}, bf16[256,512]{1,0:T(8,128)(2,1)S(1)}, u32[]{:S(2)}, u32[]{:S(2)}) collective-permute-start(bf16[256,512]{1,0:T(8,128)(2,1)S(1)} %collective-permute-done.57), channel_id=1, source_target_pairs={{0,64},{1,0},{16,80},{17,16},{32,96},{33,32},{48,112},{49,48},{64,... | collective-permute-start | bytes 786440 | tf_op jit(solution)/shard_map/ppermute | solution.py:24
  207.6 15.4 %collective-permute-start.67 = (bf16[256,512]{1,0:T(8,128)(2,1)S(1)}, bf16[256,512]{1,0:T(8,128)(2,1)S(1)}, u32[]{:S(2)}, u32[]{:S(2)}) collective-permute-start(bf16[256,512]{1,0:T(8,128)(2,1)S(1)} %get-tuple-element.51.refs_16_), channel_id=1, source_target_pairs={{0,48},{1,49},{16,0},{17,1},{32,16},{33,17},{48,32},{49,33},{64,11... | collective-permute-start | bytes 786440 | tf_op jit(solution)/shard_map/ppermute | solution.py:24
  209.6 13.9 %collective-permute-start.60 = (bf16[256,512]{1,0:T(8,128)(2,1)S(1)}, bf16[256,512]{1,0:T(8,128)(2,1)S(1)}, u32[]{:S(2)}, u32[]{:S(2)}) collective-permute-start(bf16[256,512]{1,0:T(8,128)(2,1)S(1)} %get-tuple-element.52.refs_8_), channel_id=1, source_target_pairs={{0,16},{1,17},{16,32},{17,33},{32,48},{33,49},{48,0},{49,1},{64,80... | collective-permute-start | bytes 786440 | tf_op jit(solution)/shard_map/ppermute | solution.py:24
  (45 other events, 445.2 us)
